TPU v7x, 32 devices: a whole 2x2x4 slice. The times are simulated.
32 devices in a mesh: seg: 4 (over z), grp: 4 (over y, x), pair: 2 (over core).
Axes of the slice: x: 2, y: 2, z: 4, core: 2. Of those that a mesh axis runs over, the one named last changes fastest.
Arguments:
- observations: float32 [128, 256], P(('grp', 'seg')), may hold values from -6 to 6
- masks: int32 [128, 256], P(('grp', 'seg')), may hold values 0 or 1
- gains: float32 [256], replicated, may hold values from 0.05 to 0.5
- transition: float32 [256, 256], replicated, may hold values from -1 to 1, as said below
- smoother_scale: float32 [256], replicated, may hold values from 0.995 to 0.9999
- initial_mean: float32 [256], replicated, may hold values from -8 to 8
Outputs:
- filtered: float32 [128, 256], P(('grp', 'seg'), 'pair')
- smoothed: float32 [128, 256], P(('grp', 'seg'), 'pair')
Inputs may be any that keep to these rules, and one draw needn't show every extreme that they name: Each column of transition is a unit vector scaled by a factor in (0, 1); the columns are orthogonal.
All inputs are finite; a program needn't handle non-finite values. No bound on the sum of `masks` on one device may be relied on, other than what follows from the above.
Results may differ from a plain program's by a relative error of at most 0.0003.
Values sent between devices are 32-bit elements; how exact they have to be, the bound alone decides.
No kernel may reach another device: no remote copies, remote signals or barrier semaphores. Data moves between devices by JAX's collectives and lax.ppermute only.
A program may use at most 64 MiB of HBM per device.

v0:
```python
import jax
import jax.numpy as jnp
from jax import lax
from jax.sharding import PartitionSpec as P


def entering(x, axis, combine, identity, reverse):
    size, here = (lax.axis_size(axis), lax.axis_index(axis))
    everything = jax.tree.map(lambda part: lax.all_gather(part, axis), x)
    start = jax.tree.map(
        lambda part, zero: jnp.broadcast_to(jnp.asarray(zero, part.dtype), part.shape), x, identity
    )

    def turn(k, before):
        at = size - 1 - k if reverse else k
        reached = at > here if reverse else at < here
        new = combine(before, jax.tree.map(lambda part: part[at], everything))
        return jax.tree.map(lambda a, b: jnp.where(reached, a, b), new, before)

    return lax.fori_loop(0, size, turn, start)


def spread(value, axis, source):
    kept = jnp.where(lax.axis_index(axis) == source, value, 0).astype(value.dtype)
    return lax.psum(kept, axis)


def shifted(value, axis, steps):
    count = lax.axis_size(axis)
    initial, last = (max(0, -steps), min(count, count - steps))
    return lax.ppermute(value, axis, [(source, source + steps) for source in range(initial, last)])


def compose(earlier, later_elem):
    highest = lax.Precision.HIGHEST
    matrix = jnp.dot(later_elem[0], earlier[0], precision=highest)
    offset = jnp.dot(later_elem[0], earlier[1], precision=highest) + later_elem[1]
    return (matrix, offset)


def shards(observations, masks, gains, transition, smoother_scale, initial_mean):
    highest = lax.Precision.HIGHEST
    state_width = transition.shape[0]
    day_count = observations.shape[0]
    observed = masks.astype(jnp.float32) * gains[None, :]
    retain = 1.0 - observed
    forcing = observed * observations
    smoother_gain = smoother_scale[:, None] * transition.T
    half_cols = state_width // lax.axis_size("pair")
    col_start = lax.axis_index("pair") * half_cols

    def forward_advance(position, product):
        scaled = jnp.dot(transition, product, precision=highest)
        return lax.dynamic_index_in_dim(retain, position, 0, False)[:, None] * scaled

    forward_half = lax.fori_loop(
        1,
        day_count,
        forward_advance,
        retain[0][:, None] * lax.dynamic_slice_in_dim(transition, col_start, half_cols, 1),
    )

    def gain_advance(position, product):
        return jnp.dot(smoother_gain, product, precision=highest)

    power_half = lax.fori_loop(
        1, day_count, gain_advance, lax.dynamic_slice_in_dim(smoother_gain, col_start, half_cols, 1)
    )
    fwd_matrix, gain_matrix = (
        lax.all_gather(forward_half, "pair", axis=1, tiled=True),
        lax.all_gather(power_half, "pair", axis=1, tiled=True),
    )

    def forward_run(mean_start):

        def forward_step(mean_prev, row_pair):
            retain_row, forcing_row = row_pair
            mean_next = retain_row * jnp.dot(transition, mean_prev, precision=highest) + forcing_row
            return (mean_next, mean_next)

        return lax.scan(forward_step, mean_start, (retain, forcing))

    def backward_run(smooth_end, means):

        def backward_step(smooth_next, mean_here):
            predicted = jnp.dot(transition, mean_here, precision=highest)
            smooth_here = mean_here + jnp.dot(
                smoother_gain, smooth_next - predicted, precision=highest
            )
            return (smooth_here, smooth_here)

        return lax.scan(backward_step, smooth_end, means, reverse=True)

    zeros_vec = jnp.zeros((state_width,), jnp.float32)
    identity = (jnp.eye(state_width, dtype=jnp.float32), zeros_vec)
    seg_count = lax.axis_size("seg")
    seg_index = lax.axis_index("seg")
    grp_count = lax.axis_size("grp")
    grp_index = lax.axis_index("grp")
    fwd_offset, unused = forward_run(zeros_vec)
    own_forward = (fwd_matrix, fwd_offset)
    before = entering(own_forward, "seg", compose, identity, False)
    through = compose(before, own_forward)
    group_total = (
        spread(through[0], "seg", seg_count - 1),
        spread(through[1], "seg", seg_count - 1),
    )
    entry_mean = initial_mean
    for rounds in range(1, grp_count):
        leaving = jnp.dot(group_total[0], entry_mean, precision=highest) + group_total[1]
        arrived = shifted(leaving, "grp", 1)
        entry_mean = jnp.where(grp_index == rounds, arrived, entry_mean)
    start_mean = jnp.dot(before[0], entry_mean, precision=highest) + before[1]
    last_mean, filtered = forward_run(start_mean)
    back_offset, unused_two = backward_run(zeros_vec, filtered)
    is_last = jnp.logical_and(seg_index == seg_count - 1, grp_index == grp_count - 1)
    boundary = jnp.dot(transition, last_mean, precision=highest)
    own_backward = (
        jnp.where(is_last, 0.0, gain_matrix),
        jnp.where(
            is_last, jnp.dot(gain_matrix, boundary, precision=highest) + back_offset, back_offset
        ),
    )
    behind = entering(own_backward, "seg", compose, identity, True)
    through_back = compose(behind, own_backward)
    back_total = (spread(through_back[0], "seg", 0), spread(through_back[1], "seg", 0))
    exit_smooth = zeros_vec
    for rounds in range(1, grp_count):
        leaving_back = jnp.dot(back_total[0], exit_smooth, precision=highest) + back_total[1]
        arrived_back = shifted(leaving_back, "grp", -1)
        exit_smooth = jnp.where(grp_index == grp_count - 1 - rounds, arrived_back, exit_smooth)
    smooth_end = jnp.dot(behind[0], exit_smooth, precision=highest) + behind[1]
    smooth_end = jnp.where(is_last, boundary, smooth_end)
    unused_three, smoothed = backward_run(smooth_end, filtered)
    out_cols = state_width // lax.axis_size("pair")
    out_start = lax.axis_index("pair") * out_cols
    filtered_part = lax.dynamic_slice_in_dim(filtered, out_start, out_cols, 1)
    smoothed_part = lax.dynamic_slice_in_dim(smoothed, out_start, out_cols, 1)
    return (filtered_part, smoothed_part)


def solution(mesh):
    return jax.shard_map(
        shards,
        mesh=mesh,
        in_specs=(P(("grp", "seg"), None), P(("grp", "seg"), None), P(), P(), P(), P()),
        out_specs=(P(("grp", "seg"), "pair"), P(("grp", "seg"), "pair")),
        check_vma=False,
    )
```

profile of v0, /device:TPU:0, one launch (start us, length us, event | category | flops | bytes accessed | tf_op | source)
XLA Modules:
  0.0 218.8 jit_solution(14768913008447524611)
XLA Ops:
  9.6 3.1 %while.113 = (s32[]{:T(128)}, f32[256,128]{1,0:T(8,128)S(1)}, f32[8,256]{1,0:T(8,128)S(1)}, f32[256,256]{1,0:T(8,128)S(1)}, s32[]{:T(128)}, /*index=5*/s32[]{:T(128)}, s32[]{:T(128)}) while((s32[]{:T(128)}, f32[256,128]{1,0:T(8,128)S(1)}, f32[8,256]{1,0:T(8,128)S(1)}, f32[256,256]{1,0:T(8,128)S(1)}, s32[]{:T(128)}, /*index=5*/s32[]{:T(128)}, ...), condition=%wide.region_1.2_spmd, body=%wide.region_0.1_spmd.sunk | while | flops 100696064 | bytes 789627 | solution.py:56
  12.7 2.3 %all_gather.30 = f32[256,256]{1,0:T(8,128)} all-gather(f32[256,128]{1,0:T(8,128)S(1)} %get-tuple-element.679), channel_id=1, replica_groups=mesh['seg'=4,'grp'=4,'pair'=2] {'pair'}, dimensions={1}, use_global_device_ids=true | all-gather | bytes 393216 | tf_op jit(solution)/shard_map/all_gather | solution.py:70
  15.0 2.9 %while.117 = (s32[]{:T(128)}, f32[256]{0:T(256)S(1)}, f32[8,256]{1,0:T(8,128)S(1)}, f32[256,256]{1,0:T(8,128)S(1)}, f32[8,256]{1,0:T(8,128)S(1)}, /*index=5*/s32[]{:T(128)}, s32[]{:T(128)}) while((s32[]{:T(128)}, f32[256]{0:T(256)S(1)}, f32[8,256]{1,0:T(8,128)S(1)}, f32[256,256]{1,0:T(8,128)S(1)}, f32[8,256]{1,0:T(8,128)S(1)}, ...), condition=%wide.region_3.4_spmd.clone, body=%wide.region_2.3_spmd.clone.sunk | while | flops 787203 | bytes 274523 | solution.py:81
  18.0 12.5 %all-gather.4 = f32[4,1,256]{2,1,0:T(1,128)S(1)} all-gather(f32[1,1,256]{2,1,0:T(1,128)S(1)} %bitcast.253), channel_id=3, replica_groups=mesh['seg'=4,'grp'=4,'pair'=2] {'seg'}, dimensions={0}, use_global_device_ids=true | all-gather | bytes 5120 | tf_op jit(solution)/shard_map/all_gather | solution.py:9
  32.2 13.5 %all-gather.9.cloned.1.call-done = f32[1024,256]{1,0:T(8,128)} async-done(((f32[256,256]{1,0:T(8,128)}), f32[1024,256]{1,0:T(8,128)}) %all-gather.9.cloned.1.call-update) | async-done | bytes 1048592 | tf_op jit(solution)/shard_map/all_gather | solution.py:9
  45.7 10.8 %while.118 = (s32[]{:T(128)}, f32[256,256]{1,0:T(8,128)S(1)}, f32[256]{0:T(256)S(1)}, s32[]{:T(128)}, f32[4,256,256]{2,1,0:T(8,128)}, /*index=5*/f32[4,256]{1,0:T(4,128)S(1)}, s32[]{:T(128)}, s32[]{:T(128)}) while((s32[]{:T(128)}, f32[256,256]{1,0:T(8,128)S(1)}, f32[256]{0:T(256)S(1)}, s32[]{:T(128)}, f32[4,256,256]{2,1,0:T(8,128)}, ...), condition=%wide.region_5.6_spmd.clone, body=%wide.region_4.5_spmd.clone.sunk | while | flops 202179584 | bytes 1846383 | solution.py:20
  58.1 10.2 %psum.29 = f32[256]{0:T(256)S(1)} all-reduce(f32[256]{0:T(256)S(1)} %add_select_fusion.5), channel_id=1, replica_groups=mesh['seg'=4,'grp'=4,'pair'=2] {'seg'}, use_global_device_ids=true, to_apply=%region_7.8 | all-reduce | flops 256 | bytes 2048 | tf_op jit(solution)/shard_map/psum | solution.py:25
  68.3 24.4 %all-reduce.3.cloned.1.call-done = f32[256,256]{1,0:T(8,128)} async-done(((f32[256,256]{1,0:T(8,128)}), f32[256,256]{1,0:T(8,128)}) %all-reduce.3.cloned.1.call-update) | async-done | bytes 262160 | tf_op jit(solution)/shard_map/psum | solution.py:25
  94.0 3.4 %collective-permute-start = (f32[256]{0:T(256)S(1)}, f32[256]{0:T(256)S(1)}, u32[]{:S(2)}, u32[]{:S(2)}) collective-permute-start(f32[256]{0:T(256)S(1)} %add.218), channel_id=1, source_target_pairs={{0,2},{2,4},{4,6},{1,3},{3,5},{5,7},{8,10},{10,12},{12,14},{9,11},... | collective-permute-start | bytes 3080 | tf_op jit(solution)/shard_map/ppermute | solution.py:31
  97.4 2.9 %while.115 = (s32[]{:T(128)}, f32[256,128]{1,0:T(8,128)S(1)}, f32[256,256]{1,0:T(8,128)S(1)}, s32[]{:T(128)}) while((s32[]{:T(128)}, f32[256,128]{1,0:T(8,128)S(1)}, f32[256,256]{1,0:T(8,128)S(1)}, s32[]{:T(128)}) %tuple.227), condition=%wide.region_11.12_spmd, body=%wide.region_10.11_spmd.sunk | while | flops 100663296 | bytes 786485 | solution.py:66
  100.6 3.4 %collective-permute-start.1 = (f32[256]{0:T(256)S(1)}, f32[256]{0:T(256)S(1)}, u32[]{:S(2)}, u32[]{:S(2)}) collective-permute-start(f32[256]{0:T(256)S(1)} %add.219), channel_id=1, source_target_pairs={{0,2},{2,4},{4,6},{1,3},{3,5},{5,7},{8,10},{10,12},{12,14},{9,11},... | collective-permute-start | bytes 3080 | tf_op jit(solution)/shard_map/ppermute | solution.py:31
  104.1 2.0 all_gather.35
  106.3 3.5 %collective-permute-start.2 = (f32[256]{0:T(256)S(1)}, f32[256]{0:T(256)S(1)}, u32[]{:S(2)}, u32[]{:S(2)}) collective-permute-start(f32[256]{0:T(256)S(1)} %add.220), channel_id=1, source_target_pairs={{0,2},{2,4},{4,6},{1,3},{3,5},{5,7},{8,10},{10,12},{12,14},{9,11},... | collective-permute-start | bytes 3080 | tf_op jit(solution)/shard_map/ppermute | solution.py:31
  111.5 3.2 %while.114 = (s32[]{:T(128)}, f32[256]{0:T(256)S(1)}, f32[8,256]{1,0:T(8,128)S(1)}, f32[8,256]{1,0:T(8,128)S(1)}, f32[256,256]{1,0:T(8,128)S(1)}, /*index=5*/f32[8,256]{1,0:T(8,128)S(1)}, s32[]{:T(128)}, s32[]{:T(128)}) while((s32[]{:T(128)}, f32[256]{0:T(256)S(1)}, f32[8,256]{1,0:T(8,128)S(1)}, f32[8,256]{1,0:T(8,128)S(1)}, ...), condition=%wide.region_9.10_spmd, body=%wide.region_8.9_spmd.sunk | while | flops 786946 | bytes 274525 | solution.py:81
  114.7 5.3 %while.119 = (s32[]{:T(128)}, f32[256]{0:T(256)S(1)}, f32[8,256]{1,0:T(8,128)S(1)}, f32[256,256]{1,0:T(8,128)S(1)}, f32[256,256]{1,0:T(8,128)S(1)}, /*index=5*/s32[]{:T(128)}, s32[]{:T(128)}, s32[]{:T(128)}) while((s32[]{:T(128)}, f32[256]{0:T(256)S(1)}, f32[8,256]{1,0:T(8,128)S(1)}, f32[256,256]{1,0:T(8,128)S(1)}, ...), condition=%wide.region_13.14_spmd.clone, body=%wide.region_12.13_spmd.clone.sunk | while | flops 1573636 | bytes 536687 | solution.py:92
  120.7 10.2 %all-gather.5 = f32[4,1,256]{2,1,0:T(1,128)S(1)} all-gather(f32[1,1,256]{2,1,0:T(1,128)S(1)} %bitcast.260), channel_id=5, replica_groups=mesh['seg'=4,'grp'=4,'pair'=2] {'seg'}, dimensions={0}, use_global_device_ids=true | all-gather | bytes 5120 | tf_op jit(solution)/shard_map/all_gather | solution.py:9
  130.9 7.8 %all-gather.11.cloned.1.call-done = f32[1024,256]{1,0:T(8,128)} async-done(((f32[256,256]{1,0:T(8,128)}), f32[1024,256]{1,0:T(8,128)}) %all-gather.11.cloned.1.call-update) | async-done | bytes 1048592 | tf_op jit(solution)/shard_map/all_gather | solution.py:9
  138.7 10.9 %while.120 = (s32[]{:T(128)}, f32[256,256]{1,0:T(8,128)S(1)}, f32[256]{0:T(256)S(1)}, s32[]{:T(128)}, f32[4,256,256]{2,1,0:T(8,128)}, /*index=5*/f32[4,256]{1,0:...) while((s32[]{:T(128)}, f32[256,256]{1,0:T(8,128)S(1)}, f32[256]{0:T(256)S(1)}, ...), condition=%wide.region_15.16_spmd.clone, body=%wide.region_14.15_spmd.clone.sunk | while | flops 202179584 | bytes 1845429 | solution.py:20
  151.1 10.2 %psum.31 = f32[256]{0:T(256)S(1)} all-reduce(f32[256]{0:T(256)S(1)} %add_select_fusion.4), channel_id=1, replica_groups=mesh['seg'=4,'grp'=4,'pair'=2] {'seg'}, use_global_device_ids=true, to_apply=%region_17.18 | all-reduce | flops 256 | bytes 2048 | tf_op jit(solution)/shard_map/psum | solution.py:25
  161.3 24.7 %all-reduce.5.cloned.1.call-done = f32[256,256]{1,0:T(8,128)} async-done(((f32[256,256]{1,0:T(8,128)}), f32[256,256]{1,0:T(8,128)}) %all-reduce.5.cloned.1.call-update) | async-done | bytes 262160 | tf_op jit(solution)/shard_map/psum | solution.py:25
  188.6 4.2 %collective-permute-done.3 = f32[256]{0:T(256)S(1)} collective-permute-done((f32[256]{0:T(256)S(1)}, f32[256]{0:T(256)S(1)}, u32[]{:S(2)}, u32[]{:S(2)}) %collective-permute-start.3) | collective-permute-done | bytes 1056 | tf_op jit(solution)/shard_map/ppermute | solution.py:31
  194.4 4.5 %collective-permute-done.4 = f32[256]{0:T(256)S(1)} collective-permute-done((f32[256]{0:T(256)S(1)}, f32[256]{0:T(256)S(1)}, u32[]{:S(2)}, u32[]{:S(2)}) %collective-permute-start.4) | collective-permute-done | bytes 1056 | tf_op jit(solution)/shard_map/ppermute | solution.py:31
  200.5 5.1 %collective-permute-done.5 = f32[256]{0:T(256)S(1)} collective-permute-done((f32[256]{0:T(256)S(1)}, f32[256]{0:T(256)S(1)}, u32[]{:S(2)}, u32[]{:S(2)}) %collective-permute-start.5) | collective-permute-done | bytes 1056 | tf_op jit(solution)/shard_map/ppermute | solution.py:31
  205.9 5.8 %while.116 = (s32[]{:T(128)}, f32[256]{0:T(256)S(1)}, f32[8,256]{1,0:T(8,128)S(1)}, f32[8,256]{1,0:T(8,128)S(1)}, f32[256,256]{1,0:T(8,128)S(1)}, /*index=5*/f32...) while((s32[]{:T(128)}, f32[256]{0:T(256)S(1)}, f32[8,256]{1,0:T(8,128)S(1)}, f32[8,256]{1,0:T(8,128)S(1)}, ...), condition=%wide.region_19.20_spmd, body=%wide.region_18.19_spmd.sunk | while | flops 1573379 | bytes 538737 | solution.py:92
  (320 shorter events, 60.7 us)
Async XLA Ops:
  7.2 0.7 copy-start.8
  7.2 2.4 %copy-start = (f32[256,256]{1,0:T(8,128)S(1)}, f32[256,256]{1,0:T(8,128)}, u32[]{:S(2)}) copy-start(f32[256,256]{1,0:T(8,128)} %param.25) | copy-start | bytes 786436
  7.2 38.5 %all-gather.9.cloned.1.call-start = ((), (), s32[]{:S(2)}) async-start(), calls=%async_computation.2 | async-start | bytes 1310720 | tf_op jit(solution)/shard_map/all_gather | solution.py:9
  14.9 77.8 %all-reduce.3.cloned.1.call-start = ((), (), s32[]{:S(2)}) async-start(), calls=%async_computation | async-start | bytes 524288 | tf_op jit(solution)/shard_map/psum | solution.py:25
  30.6 0.7 copy-start.1
  31.3 0.7 copy-start.9
  32.1 13.6 %copy-start.3 = (f32[256,256]{1,0:T(8,128)S(1)}, f32[256,256]{1,0:T(8,128)}, u32[]{:S(2)}) copy-start(f32[256,256]{1,0:T(8,128)} %copy-done.1) | copy-start | bytes 786436
  45.7 10.9 %copy-start.5 = (f32[256,256]{1,0:T(8,128)S(1)}, f32[256,256]{1,0:T(8,128)}, u32[]{:S(2)}) copy-start(f32[256,256]{1,0:T(8,128)} %all_gather.30) | copy-start | bytes 786436
  57.7 81.0 %all-gather.11.cloned.1.call-start = ((), (), s32[]{:S(2)}) async-start(), calls=%async_computation.3 | async-start | bytes 1310720 | tf_op jit(solution)/shard_map/all_gather | solution.py:9
  68.3 24.4 %copy-start.10 = (f32[256]{0:T(256)S(1)}, f32[256]{0:T(256)}, u32[]{:S(2)}) copy-start(f32[256]{0:T(256)} %param.27) | copy-start | bytes 3076
  94.0 6.3 %collective-permute-start = (f32[256]{0:T(256)S(1)}, f32[256]{0:T(256)S(1)}, u32[]{:S(2)}, u32[]{:S(2)}) collective-permute-start(f32[256]{0:T(256)S(1)} %add.218), channel_id=1, source_target_pairs={{0,2},{2,4},{4,6},{1,3},{3,5},{5,7},{8,10},{10,12},{12,14},{9,11},... | collective-permute-start | bytes 3080 | tf_op jit(solution)/shard_map/ppermute | solution.py:31
  97.4 3.0 %copy-start.6 = (f32[256,256]{1,0:T(8,128)S(1)}, f32[256,256]{1,0:T(8,128)}, u32[]{:S(2)}) copy-start(f32[256,256]{1,0:T(8,128)} %all-reduce.3.cloned.1.call-done) | copy-start | bytes 786436
  100.6 5.4 %collective-permute-start.1 = (f32[256]{0:T(256)S(1)}, f32[256]{0:T(256)S(1)}, u32[]{:S(2)}, u32[]{:S(2)}) collective-permute-start(f32[256]{0:T(256)S(1)} %add.219), channel_id=1, source_target_pairs={{0,2},{2,4},{4,6},{1,3},{3,5},{5,7},{8,10},{10,12},{12,14},{9,11},... | collective-permute-start | bytes 3080 | tf_op jit(solution)/shard_map/ppermute | solution.py:31
  106.3 4.8 %collective-permute-start.2 = (f32[256]{0:T(256)S(1)}, f32[256]{0:T(256)S(1)}, u32[]{:S(2)}, u32[]{:S(2)}) collective-permute-start(f32[256]{0:T(256)S(1)} %add.220), channel_id=1, source_target_pairs={{0,2},{2,4},{4,6},{1,3},{3,5},{5,7},{8,10},{10,12},{12,14},{9,11},... | collective-permute-start | bytes 3080 | tf_op jit(solution)/shard_map/ppermute | solution.py:31
  110.6 75.3 %all-reduce.5.cloned.1.call-start = ((), (), s32[]{:S(2)}) async-start(), calls=%async_computation.1 | async-start | bytes 524288 | tf_op jit(solution)/shard_map/psum | solution.py:25
  120.0 18.7 %copy-start.2 = (f32[256,256]{1,0:T(8,128)S(1)}, f32[256,256]{1,0:T(8,128)}, u32[]{:S(2)}) copy-start(f32[256,256]{1,0:T(8,128)} %copy-done.1) | copy-start | bytes 786436
  138.7 10.9 %copy-start.4 = (f32[256,256]{1,0:T(8,128)S(1)}, f32[256,256]{1,0:T(8,128)}, u32[]{:S(2)}) copy-start(f32[256,256]{1,0:T(8,128)} %broadcast_select_fusion.3) | copy-start | bytes 786436
  185.9 6.8 %copy-start.7 = (f32[256,256]{1,0:T(8,128)S(1)}, f32[256,256]{1,0:T(8,128)}, u32[]{:S(2)}) copy-start(f32[256,256]{1,0:T(8,128)} %all-reduce.5.cloned.1.call-done) | copy-start | bytes 786436
  187.2 5.5 %collective-permute-start.3 = (f32[256]{0:T(256)S(1)}, f32[256]{0:T(256)S(1)}, u32[]{:S(2)}, u32[]{:S(2)}) collective-permute-start(f32[256]{0:T(256)S(1)} %add.224), channel_id=1, source_target_pairs={{2,0},{4,2},{6,4},{3,1},{5,3},{7,5},{10,8},{12,10},{14,12},{11,9},... | collective-permute-start | bytes 3080 | tf_op jit(solution)/shard_map/ppermute | solution.py:31
  193.0 5.9 %collective-permute-start.4 = (f32[256]{0:T(256)S(1)}, f32[256]{0:T(256)S(1)}, u32[]{:S(2)}, u32[]{:S(2)}) collective-permute-start(f32[256]{0:T(256)S(1)} %add.225), channel_id=1, source_target_pairs={{2,0},{4,2},{6,4},{3,1},{5,3},{7,5},{10,8},{12,10},{14,12},{11,9},... | collective-permute-start | bytes 3080 | tf_op jit(solution)/shard_map/ppermute | solution.py:31
  199.2 6.4 %collective-permute-start.5 = (f32[256]{0:T(256)S(1)}, f32[256]{0:T(256)S(1)}, u32[]{:S(2)}, u32[]{:S(2)}) collective-permute-start(f32[256]{0:T(256)S(1)} %add.226), channel_id=1, source_target_pairs={{2,0},{4,2},{6,4},{3,1},{5,3},{7,5},{10,8},{12,10},{14,12},{11,9},... | collective-permute-start | bytes 3080 | tf_op jit(solution)/shard_map/ppermute | solution.py:31
Sparse Core Ops, SparseCore 0:
  15.1 30.6 all-gather.8
  57.8 34.8 all-reduce.2
  110.7 27.9 all-gather.10
  150.8 35.0 all-reduce.4
where the time goes:
time: 220 us; the launch traced here: 219 us
  waiting for transfers between devices  84.6 us (38%)
  blocking collectives  47.4 us (22%)
  matrix products  46.8 us (21%)
  starting transfers between devices  14.5 us (7%)
  between operations  14.5 us (7%)
  local copies, waits for them, and re-layouts  5.48 us (2%)
  other arithmetic  3.67 us (2%)
    psum x2, waiting for transfers between devices, spread(): return lax.psum(kept, axis)  49 us
    all_gather x2, blocking collectives, entering(): everything = jax.tree.map(lambda part: lax.all_gather(part, axis), x)  22.7 us
    all_gather x2, waiting for transfers between devices, entering(): everything = jax.tree.map(lambda part: lax.all_gather(part, axis), x)  21.3 us
    psum x2, blocking collectives, spread(): return lax.psum(kept, axis)  20.5 us
    ppermute x6, starting transfers between devices, shifted(): lax.ppermute(value, axis, [(source, source + steps) for source in range(i...  14.3 us
    ppermute x6, waiting for transfers between devices, shifted(): lax.ppermute(value, axis, [(source, source + steps) for source in range(i...  14.2 us
    dot_general x10, matrix products, compose(): matrix = jnp.dot(later_elem[0], earlier[0], precision=highest)  12.9 us
    dot_general x10, matrix products, compose(): jnp.dot(later_elem[0], earlier[1], precision=highest) + later_elem[1]  10.4 us
  transfers between devices with their start and end apart: 10, of which 8 were waited for; matrix products, arithmetic and copies ran while one was open for 7% of the time, Pallas kernels for 0%

commit v1 on v0

v1 whole, which is shorter than its diff:
```python
import functools
import jax
import jax.numpy as jnp
from jax import lax
from jax.experimental import pallas as pl
from jax.experimental.pallas import tpu as pltpu
from jax.sharding import PartitionSpec as P

HIGHEST = lax.Precision.HIGHEST
F32 = jnp.float32
BF16 = jnp.bfloat16
ROWS = 8
PARAMS = pltpu.CompilerParams(vmem_limit_bytes=20 * 2**20)


def split(x):
    high = x.astype(BF16)
    return high, (x - high.astype(F32)).astype(BF16)


def dot3(x, high, low):
    x_high, x_low = split(x)
    n = x.shape[0]
    both = jnp.dot(jnp.concatenate([x_high, x_low], 0), high, preferred_element_type=F32)
    return both[:n] + (both[n:] + jnp.dot(x_high, low, preferred_element_type=F32))


def powers_kernel(t_ref, scale_ref, th_ref, tl_ref, high_ref, low_ref, keep_ref):
    count = high_ref.shape[0]
    t = t_ref[...]
    t_t = jnp.transpose(t)
    th_ref[...], tl_ref[...] = split(t_t)
    keep_ref[...] = 1.0 - scale_ref[...] * jnp.sum(t * t, axis=0, keepdims=True)
    power = t * scale_ref[...]
    for k in range(count):
        high_ref[k], low_ref[k] = split(power)
        if k + 1 < count:
            power = jnp.dot(power, power, precision=HIGHEST, preferred_element_type=F32)


def smoother_kernel(
    here_ref, data_ref, gains_ref, mean_ref, th_ref, tl_ref, high_ref, low_ref, keep_ref,
    filt_ref, smooth_ref, s_ref,
):
    blocks = data_ref.shape[0]
    width = data_ref.shape[-1]
    days = blocks * ROWS
    here = here_ref[0]

    @pl.when(here_ref[1] > 0)
    def work():
        row = lax.broadcasted_iota(jnp.int32, (ROWS, width), 0)

        def forward(block, x):
            at = lax.bitwise_xor(block, here)
            observed = data_ref[at, 1] * gains_ref[...]
            retain = 1.0 - observed
            forcing = observed * data_ref[at, 0]
            out = jnp.zeros((ROWS, width), F32)
            for k in range(ROWS):
                x = retain[k : k + 1] * dot3(x, th_ref[...], tl_ref[...]) + forcing[k : k + 1]
                out = jnp.where(row == k, x, out)
            s_ref[pl.ds(pl.multiple_of(block * ROWS, ROWS), ROWS)] = out
            return x

        last = lax.fori_loop(
            0, blocks, forward, jnp.broadcast_to(mean_ref[...], (ROWS, width))
        )
        own = pl.ds(pl.multiple_of(here * ROWS, ROWS), ROWS)
        filt_ref[...] = s_ref[own]
        boundary = dot3(last, th_ref[...], tl_ref[...])
        entering = dot3(boundary, high_ref[0], low_ref[0])
        every = pl.ds(0, days)
        s_ref[every] = s_ref[every] * keep_ref[...]
        tail = pl.ds(days - ROWS, ROWS)
        s_ref[tail] = s_ref[tail] + jnp.where(row == ROWS - 1, entering, 0.0)
        s_ref[pl.ds(days, days)] = jnp.zeros((days, width), F32)
        step, k = 1, 0
        while step < ROWS:
            s_ref[every] = s_ref[every] + dot3(s_ref[pl.ds(step, days)], high_ref[k], low_ref[k])
            step, k = 2 * step, k + 1
        k = high_ref.shape[0] - 1
        step = days // 2
        while step >= ROWS:
            base = pl.multiple_of(here * ROWS, ROWS)
            s_ref[pl.ds(base, step)] = s_ref[pl.ds(base, step)] + dot3(
                s_ref[pl.ds(base + step, step)], high_ref[k], low_ref[k]
            )
            step, k = step // 2, k - 1
        smooth_ref[...] = s_ref[own]

    @pl.when(here_ref[1] == 0)
    def idle():
        filt_ref[...] = jnp.zeros(filt_ref.shape, F32)
        smooth_ref[...] = jnp.zeros(smooth_ref.shape, F32)


def swap(x, axis, flip):
    return lax.ppermute(x, axis, [(i, i ^ flip) for i in range(lax.axis_size(axis))])


def shards(observations, masks, gains, transition, smoother_scale, initial_mean):
    width = transition.shape[0]
    seg_count, grp_count = lax.axis_size("seg"), lax.axis_size("grp")
    blocks = seg_count * grp_count
    days = blocks * ROWS
    vmem = pl.BlockSpec(memory_space=pltpu.VMEM)
    smem = pl.BlockSpec(memory_space=pltpu.SMEM)
    count = days.bit_length() - 1
    scale_row = smoother_scale[None, :]
    th, tl, high, low, keep = pl.pallas_call(
        powers_kernel,
        out_shape=(
            jax.ShapeDtypeStruct((width, width), BF16),
            jax.ShapeDtypeStruct((width, width), BF16),
            jax.ShapeDtypeStruct((count, width, width), BF16),
            jax.ShapeDtypeStruct((count, width, width), BF16),
            jax.ShapeDtypeStruct((1, width), F32),
        ),
        in_specs=[vmem] * 2,
        out_specs=[vmem] * 5,
        compiler_params=PARAMS,
    )(transition, scale_row)
    data = jnp.stack([observations, masks.astype(F32)])[None]
    for axis, size in (("seg", seg_count), ("grp", grp_count)):
        flip = 1
        while flip < size:
            data = jnp.concatenate([data, swap(data, axis, flip)], 0)
            flip *= 2
    pair = lax.axis_index("pair")
    here = lax.axis_index("grp") * seg_count + lax.axis_index("seg")
    filtered, smoothed = pl.pallas_call(
        smoother_kernel,
        out_shape=(jax.ShapeDtypeStruct((ROWS, width), F32),) * 2,
        in_specs=[smem] + [vmem] * 8,
        out_specs=[vmem] * 2,
        scratch_shapes=[pltpu.VMEM((2 * days, width), F32)],
        compiler_params=PARAMS,
    )(jnp.stack([here, pair]).astype(jnp.int32), data, gains[None, :], initial_mean[None, :], th, tl, high, low, keep)
    half = width // lax.axis_size("pair")
    both = jnp.concatenate([filtered, smoothed], 0)
    got = lax.ppermute(both[:, :half], "pair", [(0, 1), (1, 0)])
    mine = jnp.where(pair == 1, both[:, half:], got)
    return mine[:ROWS], mine[ROWS:]


def solution(mesh):
    return jax.shard_map(
        shards,
        mesh=mesh,
        in_specs=(P(("grp", "seg"), None), P(("grp", "seg"), None), P(), P(), P(), P()),
        out_specs=(P(("grp", "seg"), "pair"), P(("grp", "seg"), "pair")),
        check_vma=False,
    )
```

time: 220 us -> 40.6 us (0.18)
  waiting for transfers between devices: 84.6 us -> 8.75 us
  blocking collectives: 47.4 us -> 0 us
  matrix products: 46.8 us -> 0 us
  between operations: 14.5 us -> 0.72 us
  starting transfers between devices: 14.5 us -> 23.4 us
  Pallas kernels: 0 us -> 3.77 us
  other arithmetic: 3.67 us -> 0.81 us
  local copies, waits for them, and re-layouts: 5.48 us -> 2.94 us
    psum x2 -> x0, waiting for transfers between devices: 49 us -> none  [spread(): return lax.psum(kept, axis)]
    dot_general x92 -> x0, matrix products: 46.8 us -> none  [the longest x10 12.9 us: compose(): matrix = jnp.dot(later_elem[0], earlier[0], precision=highest)]
    all_gather x4 -> x0, blocking collectives: 27 us -> none  [the longest x2 22.7 us: entering(): everything = jax.tree.map(lambda part: lax.all_gather(part, axis), x)]
    all_gather x2 -> x0, waiting for transfers between devices: 21.3 us -> none  [entering(): everything = jax.tree.map(lambda part: lax.all_gather(part, axis), x)]
    psum x2 -> x0, blocking collectives: 20.5 us -> none  [spread(): return lax.psum(kept, axis)]
    ppermute x6 -> x5, starting transfers between devices: 14.3 us -> 23.4 us  [the longest x1 14.1 us: shards(): got = lax.ppermute(both[:, :half], 'pair', [(0, 1), (1, 0)])]
    ppermute x6 -> x5, waiting for transfers between devices: 14.2 us -> 8.75 us  [the longest x4 7.92 us: swap(): lax.ppermute(x, axis, [(i, i ^ flip) for i in range(lax.axis_size(axis))])]
    pallas_call x0 -> x2, Pallas kernels: none -> 3.77 us  [the longest x1 3.22 us: shards(): pl.pallas_call(powers_kernel, out_shape=(jax.ShapeDtypeStruct((width, wid...]
  transfers between devices with their start and end apart: 10 -> 5, of which waited for: 8 -> 4; matrix products, arithmetic and copies ran while one was open for 7% -> 0% of each run, Pallas kernels for 0% -> 8%
where the time goes in v1:
time: 40.6 us; the launch traced here: 40.4 us
  starting transfers between devices  23.4 us (58%)
  waiting for transfers between devices  8.75 us (22%)
  Pallas kernels  3.77 us (9%)
  local copies, waits for them, and re-layouts  2.94 us (7%)
  other arithmetic  0.81 us (2%)
  between operations  0.72 us (2%)
    ppermute x1, starting transfers between devices, shards(): got = lax.ppermute(both[:, :half], 'pair', [(0, 1), (1, 0)])  14.1 us
    ppermute x4, starting transfers between devices, swap(): lax.ppermute(x, axis, [(i, i ^ flip) for i in range(lax.axis_size(axis))])  9.23 us
    ppermute x4, waiting for transfers between devices, swap(): lax.ppermute(x, axis, [(i, i ^ flip) for i in range(lax.axis_size(axis))])  7.92 us
    pallas_call x1, Pallas kernels, shards(): pl.pallas_call(powers_kernel, out_shape=(jax.ShapeDtypeStruct((width, wid...  3.22 us
    unnamed x14, local copies, waits for them, and re-layouts  2.32 us
    ppermute x1, waiting for transfers between devices, shards(): got = lax.ppermute(both[:, :half], 'pair', [(0, 1), (1, 0)])  0.83 us
  transfers between devices with their start and end apart: 5, of which 4 were waited for; matrix products, arithmetic and copies ran while one was open for 0% of the time, Pallas kernels for 8%

profile of v1, /device:TPU:0, one launch (start us, length us, event | category | flops | bytes accessed | tf_op | source)
XLA Modules:
  0.0 40.4 jit_solution(10764023610647939254)
XLA Ops:
  0.6 0.0 copy-start.4
  0.6 0.7 %convert_bitcast_fusion = f32[1,8,256]{2,1,0:T(8,128)S(1)} fusion(s32[8,256]{1,0:T(8,128)} %param.7), kind=kLoop, calls=%fused_computation.12 | loop fusion | flops 2048 | bytes 16384 | tf_op jit(solution)/shard_map/stack | solution.py:124
  1.3 0.0 copy-done.4
  1.4 3.1 %collective-permute-start = (f32[1,2,8,256]{3,2,1,0:T(8,128)S(1)}, f32[1,2,8,256]{3,2,1,0:T(8,128)S(1)}, u32[]{:S(2)}, u32[]{:S(2)}) collective-permute-start(f32[1,2,8,256]{3,2,1,0:T(8,128)S(1)} %maximum_bitcast_fusion), channel_id=1, source_target_pairs={{0,8},{8,0},{16,24},{24,16},{1,9},{9,1},{17,25},{25,17},{2,10},{10... | collective-permute-start | bytes 49160 | tf_op jit(solution)/shard_map/ppermute | solution.py:99
  4.4 1.7 %collective-permute-done = f32[1,2,8,256]{3,2,1,0:T(8,128)S(1)} collective-permute-done((f32[1,2,8,256]{3,2,1,0:T(8,128)S(1)}, f32[1,2,8,256]{3,2,1,0:T(8,128)S(1)}, u32[]{:S(2)}, u32[]{:S(2)}) %collective-permute-start) | collective-permute-done | bytes 16416 | tf_op jit(solution)/shard_map/ppermute | solution.py:99
  6.1 3.0 %collective-permute-start.1 = (f32[2,2,8,256]{3,2,1,0:T(8,128)S(1)}, f32[2,2,8,256]{3,2,1,0:T(8,128)S(1)}, u32[]{:S(2)}, u32[]{:S(2)}) collective-permute-start(f32[2,2,8,256]{3,2,1,0:T(8,128)S(1)} %pad_maximum_fusion.2), channel_id=1, source_target_pairs={{0,16},{8,24},{16,0},{24,8},{1,17},{9,25},{17,1},{25,9},{2,18},{10... | collective-permute-start | bytes 98312 | tf_op jit(solution)/shard_map/ppermute | solution.py:99
  9.2 0.1 pad_add_fusion.here_ref
  9.2 0.0 copy-start.1
  9.2 0.7 %copy-done.1 = f32[256]{0:T(256)S(1)} copy-done((f32[256]{0:T(256)S(1)}, f32[256]{0:T(256)}, u32[]{:S(2)}) %copy-start.1) | copy-done | bytes 1048
  9.9 0.0 copy-start
  9.9 0.9 %copy-done = f32[256,256]{1,0:T(8,128)S(1)} copy-done((f32[256,256]{1,0:T(8,128)S(1)}, f32[256,256]{1,0:T(8,128)}, u32[]{:S(2)}) %copy-start) | copy-done | bytes 262168
  10.9 3.2 %shard_map.77 = (bf16[256,256]{1,0:T(8,128)(2,1)S(1)}, bf16[256,256]{1,0:T(8,128)(2,1)S(1)}, bf16[7,256,256]{2,1,0:T(8,128)(2,1)S(1)}, bf16[7,256,256]{2,1,0:T(8,128)(2,1)S(1)}, f32[1,256]{1,0:T(1,128)S(1)}) custom-call(f32[256,256]{1,0:T(8,128)S(1)} %copy-done, f32[1,256]{1,0:T(1,128)S(1)} %bitcast.12), custom_call_target="tpu_custom_call" | custom-call | tf_op jit(solution)/shard_map/pallas_call | solution.py:111
  14.1 0.0 collective-permute-done.1
  14.1 1.6 %collective-permute-start.2 = (f32[4,2,8,256]{3,2,1,0:T(8,128)S(1)}, f32[4,2,8,256]{3,2,1,0:T(8,128)S(1)}, u32[]{:S(2)}, u32[]{:S(2)}) collective-permute-start(f32[4,2,8,256]{3,2,1,0:T(8,128)S(1)} %pad_maximum_fusion.1), channel_id=1, source_target_pairs={{0,2},{2,0},{4,6},{6,4},{1,3},{3,1},{5,7},{7,5},{8,10},{10,8},{12,... | collective-permute-start | bytes 196616 | tf_op jit(solution)/shard_map/ppermute | solution.py:99
  15.7 2.8 %collective-permute-done.2 = f32[4,2,8,256]{3,2,1,0:T(8,128)S(1)} collective-permute-done((f32[4,2,8,256]{3,2,1,0:T(8,128)S(1)}, f32[4,2,8,256]{3,2,1,0:T(8,128)S(1)}, u32[]{:S(2)}, u32[]{:S(2)}) %collective-permute-start.2) | collective-permute-done | bytes 65568 | tf_op jit(solution)/shard_map/ppermute | solution.py:99
  18.5 1.6 %collective-permute-start.3 = (f32[8,2,8,256]{3,2,1,0:T(8,128)S(1)}, f32[8,2,8,256]{3,2,1,0:T(8,128)S(1)}, u32[]{:S(2)}, u32[]{:S(2)}) collective-permute-start(f32[8,2,8,256]{3,2,1,0:T(8,128)S(1)} %pad_maximum_fusion), channel_id=1, source_target_pairs={{0,4},{2,6},{4,0},{6,2},{1,5},{3,7},{5,1},{7,3},{8,12},{10,14},{12... | collective-permute-start | bytes 393224 | tf_op jit(solution)/shard_map/ppermute | solution.py:99
  20.1 3.4 %collective-permute-done.3 = f32[8,2,8,256]{3,2,1,0:T(8,128)S(1)} collective-permute-done((f32[8,2,8,256]{3,2,1,0:T(8,128)S(1)}, f32[8,2,8,256]{3,2,1,0:T(8,128)S(1)}, u32[]{:S(2)}, u32[]{:S(2)}) %collective-permute-start.3) | collective-permute-done | bytes 131104 | tf_op jit(solution)/shard_map/ppermute | solution.py:99
  23.5 0.0 copy-start.2
  23.5 0.7 %copy-done.3 = f32[256]{0:T(256)S(1)} copy-done((f32[256]{0:T(256)S(1)}, f32[256]{0:T(256)}, u32[]{:S(2)}) %copy-start.3) | copy-done | bytes 1048
  24.2 0.0 copy-done.2
  24.2 0.6 %shard_map.78 = (f32[8,256]{1,0:T(8,128)S(1)}, f32[8,256]{1,0:T(8,128)S(1)}) custom-call(s32[2]{0:T(128)S(1)} %pad_add_fusion.here_ref, f32[16,2,8,256]{3,2,1,0:T(8,128)S(1)} %constant_dynamic-update-slice_fusion.data_ref, f32[1,256]{1,0:T(1,128)S(1)} %bitcast.13, f32[1,256]{1,0:T(1,128)S(1)} %bitcast.14, bf16[256,256]{1,0:T(8,128)(2,1)S(1)} %get-tuple-element.9.th_ref, ...), custom_call_target="tpu_custom_call" | custom-call | tf_op jit(solution)/shard_map/pallas_call | solution.py:132
  24.8 14.1 %collective-permute-start.4 = (f32[16,128]{1,0:T(8,128)S(1)}, f32[16,128]{1,0:T(8,128)S(1)}, u32[]{:S(2)}, u32[]{:S(2)}) collective-permute-start(f32[16,128]{1,0:T(8,128)S(1)} %slice.17), channel_id=1, source_target_pairs={{0,1},{1,0},{2,3},{3,2},{4,5},{5,4},{6,7},{7,6},{8,9},{9,8},{10,11... | collective-permute-start | bytes 24584 | tf_op jit(solution)/shard_map/ppermute | solution.py:142
  38.9 0.8 %collective-permute-done.4 = f32[16,128]{1,0:T(8,128)S(1)} collective-permute-done((f32[16,128]{1,0:T(8,128)S(1)}, f32[16,128]{1,0:T(8,128)S(1)}, u32[]{:S(2)}, u32[]{:S(2)}) %collective-permute-start.4) | collective-permute-done | bytes 8224 | tf_op jit(solution)/shard_map/ppermute | solution.py:142
  39.8 0.6 %fusion = (f32[8,128]{1,0:T(8,128)}, f32[8,128]{1,0:T(8,128)}) fusion(f32[16,128]{1,0:T(8,128)S(1)} %slice_select_fusion), kind=kLoop, calls=%fused_computation.14 | loop fusion | bytes 16384 | tf_op jit(solution)/shard_map/slice | solution.py:144
  (14 shorter events, 0.1 us)
Async XLA Ops:
  0.6 0.7 %copy-start.4 = (f32[8,256]{1,0:T(8,128)S(1)}, f32[8,256]{1,0:T(8,128)}, u32[]{:S(2)}) copy-start(f32[8,256]{1,0:T(8,128)} %param.6) | copy-start | bytes 24580
  1.4 4.8 %collective-permute-start = (f32[1,2,8,256]{3,2,1,0:T(8,128)S(1)}, f32[1,2,8,256]{3,2,1,0:T(8,128)S(1)}, u32[]{:S(2)}, u32[]{:S(2)}) collective-permute-start(f32[1,2,8,256]{3,2,1,0:T(8,128)S(1)} %maximum_bitcast_fusion), channel_id=1, source_target_pairs={{0,8},{8,0},{16,24},{24,16},{1,9},{9,1},{17,25},{25,17},{2,10},{10... | collective-permute-start | bytes 49160 | tf_op jit(solution)/shard_map/ppermute | solution.py:99
  6.1 8.0 %collective-permute-start.1 = (f32[2,2,8,256]{3,2,1,0:T(8,128)S(1)}, f32[2,2,8,256]{3,2,1,0:T(8,128)S(1)}, u32[]{:S(2)}, u32[]{:S(2)}) collective-permute-start(f32[2,2,8,256]{3,2,1,0:T(8,128)S(1)} %pad_maximum_fusion.2), channel_id=1, source_target_pairs={{0,16},{8,24},{16,0},{24,8},{1,17},{9,25},{17,1},{25,9},{2,18},{10... | collective-permute-start | bytes 98312 | tf_op jit(solution)/shard_map/ppermute | solution.py:99
  9.2 0.7 %copy-start.1 = (f32[256]{0:T(256)S(1)}, f32[256]{0:T(256)}, u32[]{:S(2)}) copy-start(f32[256]{0:T(256)} %param.10) | copy-start | bytes 3076
  9.9 0.9 %copy-start = (f32[256,256]{1,0:T(8,128)S(1)}, f32[256,256]{1,0:T(8,128)}, u32[]{:S(2)}) copy-start(f32[256,256]{1,0:T(8,128)} %t_ref.1) | copy-start | bytes 786436
  14.1 4.3 %collective-permute-start.2 = (f32[4,2,8,256]{3,2,1,0:T(8,128)S(1)}, f32[4,2,8,256]{3,2,1,0:T(8,128)S(1)}, u32[]{:S(2)}, u32[]{:S(2)}) collective-permute-start(f32[4,2,8,256]{3,2,1,0:T(8,128)S(1)} %pad_maximum_fusion.1), channel_id=1, source_target_pairs={{0,2},{2,0},{4,6},{6,4},{1,3},{3,1},{5,7},{7,5},{8,10},{10,8},{12,... | collective-permute-start | bytes 196616 | tf_op jit(solution)/shard_map/ppermute | solution.py:99
  18.5 5.0 %collective-permute-start.3 = (f32[8,2,8,256]{3,2,1,0:T(8,128)S(1)}, f32[8,2,8,256]{3,2,1,0:T(8,128)S(1)}, u32[]{:S(2)}, u32[]{:S(2)}) collective-permute-start(f32[8,2,8,256]{3,2,1,0:T(8,128)S(1)} %pad_maximum_fusion), channel_id=1, source_target_pairs={{0,4},{2,6},{4,0},{6,2},{1,5},{3,7},{5,1},{7,3},{8,12},{10,14},{12... | collective-permute-start | bytes 393224 | tf_op jit(solution)/shard_map/ppermute | solution.py:99
  23.5 0.7 %copy-start.3 = (f32[256]{0:T(256)S(1)}, f32[256]{0:T(256)}, u32[]{:S(2)}) copy-start(f32[256]{0:T(256)} %param.11) | copy-start | bytes 3076
  23.5 0.7 %copy-start.2 = (f32[256]{0:T(256)S(1)}, f32[256]{0:T(256)}, u32[]{:S(2)}) copy-start(f32[256]{0:T(256)} %param.8) | copy-start | bytes 3076
  24.8 15.0 %collective-permute-start.4 = (f32[16,128]{1,0:T(8,128)S(1)}, f32[16,128]{1,0:T(8,128)S(1)}, u32[]{:S(2)}, u32[]{:S(2)}) collective-permute-start(f32[16,128]{1,0:T(8,128)S(1)} %slice.17), channel_id=1, source_target_pairs={{0,1},{1,0},{2,3},{3,2},{4,5},{5,4},{6,7},{7,6},{8,9},{9,8},{10,11... | collective-permute-start | bytes 24584 | tf_op jit(solution)/shard_map/ppermute | solution.py:142

commit v2 on v1

v2 whole, which is shorter than its diff:
```python
import functools
import jax
import jax.numpy as jnp
from jax import lax
from jax.experimental import pallas as pl
from jax.experimental.pallas import tpu as pltpu
from jax.sharding import PartitionSpec as P

HIGHEST = lax.Precision.HIGHEST
F32 = jnp.float32
BF16 = jnp.bfloat16
ROWS = 8
LANES = 128
BITS = 4
VMEM = pl.BlockSpec(memory_space=pltpu.VMEM)
SMEM = pl.BlockSpec(memory_space=pltpu.SMEM)
ANY = pl.BlockSpec(memory_space=pl.ANY)
HBM = pl.BlockSpec(memory_space=pltpu.HBM)


def params(mib):
    return pltpu.CompilerParams(vmem_limit_bytes=mib * 2**20)


def split(x):
    high = x.astype(BF16)
    return high, (x - high.astype(F32)).astype(BF16)


def dot3(x, high, low):
    x_high, x_low = split(x)
    n = x.shape[0]
    both = jnp.dot(jnp.concatenate([x_high, x_low], 0), high, preferred_element_type=F32)
    return both[:n] + (both[n:] + jnp.dot(x_high, low, preferred_element_type=F32))


def down_sum(x):
    for shift in (4, 2, 1):
        x = x + pltpu.roll(x, shift, 0)
    return x


def load_kernel(
    obs_hbm, mask_hbm, t_hbm, scale_hbm, gains_hbm, mean_hbm, data_ref, t_ref, rows_ref, mask_ref, in_ref, sems
):
    targets = (data_ref.at[0, 0], mask_ref, t_ref, in_ref.at[2], in_ref.at[0], in_ref.at[1])
    sources = (obs_hbm, mask_hbm, t_hbm, scale_hbm, gains_hbm, mean_hbm)
    copies = [
        pltpu.make_async_copy(source, target, sems.at[k])
        for k, (source, target) in enumerate(zip(sources, targets))
    ]
    for copy in copies:
        copy.start()
    for copy in copies:
        copy.wait()
    data_ref[0, 1] = mask_ref[...].astype(F32)
    for k in range(3):
        rows_ref[k : k + 1] = in_ref[k]


def setup_kernel(
    t_ref, in_ref, tt_ref, th_ref, tl_ref, rows_ref, kept_ref, power_ref, high_ref, low_ref
):
    width = t_ref.shape[0]
    t = t_ref[...]
    t_t = jnp.transpose(t)
    tt_ref[...] = t_t
    th_ref[...], tl_ref[...] = split(t_t)
    scale = in_ref[2:3]
    keep = 1.0 - scale * jnp.sum(t * t, axis=0, keepdims=True)
    rows_ref[...] = in_ref[...]
    rows_ref[2:3] = keep
    kept = jnp.transpose(jnp.broadcast_to(1.0 - in_ref[0:1], (ROWS, width)))
    kept_ref[...] = jnp.broadcast_to(kept[:, :1], (width, LANES))
    power = t * scale
    power_ref[...] = power
    high_ref[0], low_ref[0] = split(power)


def power_kernel(gate, in_ref, power_ref, high_ref, low_ref):
    del gate
    power = in_ref[...]
    for k in range(high_ref.shape[0]):
        power = jnp.dot(power, power, precision=HIGHEST, preferred_element_type=F32)
        high_ref[k], low_ref[k] = split(power)
    power_ref[...] = power


def smoother_kernel(steps, here_ref, data_ref, rows_ref, kept_ref, t_ref, tt_ref, th_ref, tl_ref, *refs):
    highs, lows = refs[: len(steps)], refs[len(steps) : 2 * len(steps)]
    send_ref, mine_ref, bits_ref, retain_ref, force_ref, f_ref, s_ref = refs[2 * len(steps) :]
    blocks = data_ref.shape[0]
    width = data_ref.shape[-1]
    days = blocks * ROWS
    here = here_ref[0]
    half = width // 2
    tiles = width // ROWS
    powers = [(high, low, k) for high, low, n in zip(highs, lows, steps) for k in range(n)]

    def advance(x, k):
        high, low, at = powers[k]
        return dot3(x, high[at], low[at])

    @pl.when(here_ref[1] > 0)
    def work():
        row = lax.broadcasted_iota(jnp.int32, (ROWS, width), 0)
        gains = rows_ref[0:1]
        group = min(ROWS, blocks)

        def prepare(word, carry):
            packed = jnp.zeros((ROWS, width), jnp.int32)
            for q in range(group):
                block = word * group + q
                at = lax.bitwise_xor(block, here)
                mask = data_ref[at, 1]
                observed = mask * gains
                retain_ref[block] = 1.0 - observed
                force_ref[block] = observed * data_ref[at, 0]
                even = jnp.where((row & 1) == 0, mask, 0.0).astype(jnp.int32)
                packed = packed | (even << ((row >> 1) + BITS * q))
            for shift in (4, 2):
                packed = packed | pltpu.roll(packed, shift, 0)
            bits_ref[word] = jnp.broadcast_to(jnp.transpose(packed)[:, :1], (width, LANES))
            return carry

        lax.fori_loop(0, blocks // group, prepare, 0)
        force = force_ref[...]
        ahead = dot3(force.reshape(days, width), th_ref[...], tl_ref[...])
        ahead = pltpu.roll(ahead, 1, 0).reshape(blocks, ROWS, width)
        odd = (lax.broadcasted_iota(jnp.int32, (blocks, ROWS, width), 1) & 1) == 1
        force_ref[...] = jnp.where(odd, retain_ref[...] * ahead, 0.0) + force
        f_ref[...] = jnp.zeros(f_ref.shape, F32)
        mean = rows_ref[1:2]
        f_ref[ROWS - 1 : ROWS] = mean

        def forward(block, x):
            word, first = block // group, 31 - BITS * (block % group)
            out = jnp.zeros((ROWS, width), F32)
            for k in range(0, ROWS, 2):
                left, right = x[:, :half], x[:, half:]
                total_left = jnp.zeros((ROWS, half), F32)
                total_right = total_left
                for j in range(tiles):
                    at = slice(ROWS * j, ROWS * (j + 1))
                    product = t_ref[at, :half] * left + t_ref[at, half:] * right
                    u = jnp.broadcast_to(jnp.sum(product, axis=1, keepdims=True), (ROWS, half))
                    seen = bits_ref[word, at] << (first - k // 2)
                    u = jnp.where(seen < 0, u * kept_ref[at], u)
                    total_left = total_left + tt_ref[at, :half] * u
                    total_right = total_right + tt_ref[at, half:] * u
                z = down_sum(jnp.concatenate([total_left, total_right], 1))
                x = retain_ref[block, k + 1 : k + 2] * z + force_ref[block, k + 1 : k + 2]
                out = jnp.where(row == k + 1, x, out)
            f_ref[pl.ds(pl.multiple_of(ROWS * block + ROWS, ROWS), ROWS)] = out
            return x

        lax.fori_loop(0, blocks, forward, jnp.broadcast_to(mean, (ROWS, width)))
        every = pl.ds(ROWS, days)
        ahead = dot3(f_ref[pl.ds(ROWS - 1, days + ROWS)], th_ref[...], tl_ref[...])
        boundary = ahead[days:]
        even_days = retain_ref[...].reshape(days, width) * ahead[:days] + force_ref[...].reshape(days, width)
        day = lax.broadcasted_iota(jnp.int32, (days, width), 0)
        filtered = jnp.where((day & 1) == 0, even_days, f_ref[every])
        f_ref[every] = filtered
        s_ref[pl.ds(0, days)] = filtered * rows_ref[2:3]
        s_ref[pl.ds(days, ROWS)] = jnp.where(row == 0, boundary, 0.0)
        s_ref[pl.ds(days + ROWS, days - ROWS)] = jnp.zeros((days - ROWS, width), F32)
        entering = advance(boundary, 3)
        step, k = 1, 0
        while step < ROWS:
            s_ref[pl.ds(0, days)] = s_ref[pl.ds(0, days)] + advance(s_ref[pl.ds(step, days)], k)
            step, k = 2 * step, k + 1
        tail = pl.ds(days - ROWS, ROWS)
        s_ref[tail] = s_ref[tail] + jnp.where(row == 0, entering, 0.0)
        s_ref[pl.ds(days, ROWS)] = jnp.zeros((ROWS, width), F32)
        base = pl.multiple_of(here * ROWS, ROWS)
        k = len(powers) - 1
        step = days // 2
        while step >= ROWS:
            s_ref[pl.ds(base, step)] = s_ref[pl.ds(base, step)] + advance(s_ref[pl.ds(base + step, step)], k)
            step, k = step // 2, k - 1
        own_filtered = f_ref[pl.ds(base + ROWS, ROWS)]
        own_smoothed = s_ref[pl.ds(base, ROWS)]
        send_ref[:ROWS], mine_ref[:ROWS] = own_filtered[:, :half], own_filtered[:, half:]
        send_ref[ROWS:], mine_ref[ROWS:] = own_smoothed[:, :half], own_smoothed[:, half:]

    @pl.when(here_ref[1] == 0)
    def idle():
        send_ref[...] = jnp.zeros(send_ref.shape, F32)
        mine_ref[...] = jnp.zeros(mine_ref.shape, F32)


def swap(x, axis, flip):
    return lax.ppermute(x, axis, [(i, i ^ flip) for i in range(lax.axis_size(axis))])


def shape(*dims, dtype=F32):
    return jax.ShapeDtypeStruct(dims, dtype)


def hops(mesh_shape):
    return [(axis, 1 << k) for axis in ("seg", "grp") for k in range(mesh_shape[axis].bit_length() - 1)]


def shards(observations, masks, gains, transition, smoother_scale, initial_mean):
    width = transition.shape[0]
    sizes = {axis: lax.axis_size(axis) for axis in ("seg", "grp")}
    blocks = sizes["seg"] * sizes["grp"]
    days = blocks * ROWS
    half = width // 2
    flips = hops(sizes)
    inputs = (
        observations, masks, transition, smoother_scale[None, :], gains[None, :], initial_mean[None, :]
    )
    data, t, rows = pl.pallas_call(
        load_kernel,
        out_shape=(shape(1, 2, ROWS, width), shape(width, width), shape(ROWS, width)),
        in_specs=[HBM] * 6,
        out_specs=[VMEM] * 3,
        scratch_shapes=[
            pltpu.VMEM((ROWS, width), jnp.int32), pltpu.VMEM((3, 1, width), F32), pltpu.SemaphoreType.DMA((6,))
        ],
        compiler_params=params(4),
    )(*(pltpu.with_memory_space_constraint(x, pltpu.HBM) for x in inputs))
    tt, th, tl, rows, kept, power, high, low = pl.pallas_call(
        setup_kernel,
        out_shape=(
            shape(width, width),
            shape(width, width, dtype=BF16), shape(width, width, dtype=BF16),
            shape(ROWS, width), shape(width, LANES), shape(width, width),
            shape(1, width, width, dtype=BF16), shape(1, width, width, dtype=BF16),
        ),
        in_specs=[VMEM] * 2,
        out_specs=[VMEM] * 8,
        compiler_params=params(8),
    )(t, rows)
    highs, lows, steps = [high], [low], [1]
    left = days.bit_length() - 2
    for k, (axis, flip) in enumerate(flips):
        if k > 0:
            count = -(-left // (len(flips) - k))
            left -= count
            power, high, low = pl.pallas_call(
                power_kernel,
                out_shape=(
                    shape(width, width),
                    shape(count, width, width, dtype=BF16),
                    shape(count, width, width, dtype=BF16),
                ),
                in_specs=[ANY, VMEM],
                out_specs=[VMEM] * 3,
                compiler_params=params(8),
            )(data, power)
            highs.append(high)
            lows.append(low)
            steps.append(count)
        other = swap(data, axis, flip)
        data = jnp.concatenate([data, other], 0)
    pair = lax.axis_index("pair")
    here = lax.axis_index("grp") * sizes["seg"] + lax.axis_index("seg")
    send, mine = pl.pallas_call(
        functools.partial(smoother_kernel, steps),
        out_shape=(shape(2 * ROWS, half),) * 2,
        in_specs=[SMEM] + [VMEM] * (7 + 2 * len(steps)),
        out_specs=[VMEM] * 2,
        scratch_shapes=[
            pltpu.VMEM((max(1, blocks // ROWS), width, LANES), jnp.int32),
            pltpu.VMEM((blocks, ROWS, width), F32),
            pltpu.VMEM((blocks, ROWS, width), F32),
            pltpu.VMEM((days + 2 * ROWS, width), F32),
            pltpu.VMEM((2 * days, width), F32),
        ],
        compiler_params=params(12 + blocks // 8),
    )(jnp.stack([here, pair]).astype(jnp.int32), data, rows, kept, t, tt, th, tl, *highs, *lows)
    got = lax.ppermute(send, "pair", [(0, 1), (1, 0)])
    out = jnp.where(pair == 1, mine, got)
    return out[:ROWS], out[ROWS:]


def solution(mesh):
    return jax.shard_map(
        shards,
        mesh=mesh,
        in_specs=(P(("grp", "seg"), None), P(("grp", "seg"), None), P(), P(), P(), P()),
        out_specs=(P(("grp", "seg"), "pair"), P(("grp", "seg"), "pair")),
        check_vma=False,
    )
```

time: 40.6 us -> 30.5 us (0.75)
  starting transfers between devices: 23.4 us -> 16.2 us
  local copies, waits for them, and re-layouts: 2.94 us -> 0.64 us
  Pallas kernels: 3.77 us -> 5.85 us
  waiting for transfers between devices: 8.75 us -> 6.88 us
  other arithmetic: 0.81 us -> 0.08 us
    ppermute x1, starting transfers between devices: 14.1 us -> 6.23 us  [shards(): got = lax.ppermute(send, 'pair', [(0, 1), (1, 0)])]
    unnamed x14 -> x3, local copies, waits for them, and re-layouts: 2.32 us -> 0.02 us
    pallas_call x2 -> x6, Pallas kernels: 3.77 us -> 5.85 us  [the longest x3 3.96 us: shards(): pl.pallas_call(power_kernel, out_shape=(shape(width, width), shape(count,...]
    ppermute x4, waiting for transfers between devices: 7.92 us -> 6.05 us  [swap(): lax.ppermute(x, axis, [(i, i ^ flip) for i in range(lax.axis_size(axis))])]
    ppermute x4, starting transfers between devices: 9.23 us -> 9.96 us  [swap(): lax.ppermute(x, axis, [(i, i ^ flip) for i in range(lax.axis_size(axis))])]
    another operation x1 -> x0, other arithmetic: 0.71 us -> none  [shards(): data = jnp.stack([observations, masks.astype(F32)])[None]]
  transfers between devices with their start and end apart: 5 -> 5, of which waited for: 4 -> 4; matrix products, arithmetic and copies ran while one was open for 0% -> 0% of each run, Pallas kernels for 8% -> 14%
where the time goes in v2:
time: 30.5 us; the launch traced here: 30.3 us
  starting transfers between devices  16.2 us (53%)
  waiting for transfers between devices  6.88 us (23%)
  Pallas kernels  5.85 us (19%)
  between operations  0.7 us (2%)
  local copies, waits for them, and re-layouts  0.64 us (2%)
    ppermute x4, starting transfers between devices, swap(): lax.ppermute(x, axis, [(i, i ^ flip) for i in range(lax.axis_size(axis))])  9.96 us
    ppermute x1, starting transfers between devices, shards(): got = lax.ppermute(send, 'pair', [(0, 1), (1, 0)])  6.23 us
    ppermute x4, waiting for transfers between devices, swap(): lax.ppermute(x, axis, [(i, i ^ flip) for i in range(lax.axis_size(axis))])  6.05 us
    pallas_call x3, Pallas kernels, shards(): pl.pallas_call(power_kernel, out_shape=(shape(width, width), shape(count,...  3.96 us
    pallas_call x1, Pallas kernels, shards(): pl.pallas_call(load_kernel, out_shape=(shape(1, 2, ROWS, width), shape(wi...  1.04 us
    ppermute x1, waiting for transfers between devices, shards(): got = lax.ppermute(send, 'pair', [(0, 1), (1, 0)])  0.83 us
  transfers between devices with their start and end apart: 5, of which 4 were waited for; matrix products, arithmetic and copies ran while one was open for 0% of the time, Pallas kernels for 14%

profile of v2, /device:TPU:0, one launch (start us, length us, event | category | flops | bytes accessed | tf_op | source)
XLA Modules:
  0.0 30.3 jit_solution(12752974642687605119)
XLA Ops:
  0.6 1.0 %shard_map.77 = (f32[1,2,8,256]{3,2,1,0:T(8,128)S(1)}, f32[256,256]{1,0:T(8,128)S(1)}, f32[8,256]{1,0:T(8,128)S(1)}) custom-call(f32[8,256]{1,0:T(8,128)} %obs_hbm.1, s32[8,256]{1,0:T(8,128)} %mask_hbm.1, f32[256,256]{1,0:T(8,128)} %t_hbm.1, f32[1,256]{1,0:T(1,128)} %bitcast.5, f32[1,256]{1,0:T(1,128)} %bitcast.6, f32[1,256]{1,0:T(1,128)} %bitcast.7), custom_call_target="tpu_custom_call" | custom-call | tf_op jit(solution)/shard_map/pallas_call | solution.py:215
  1.7 3.1 %collective-permute-start = (f32[1,2,8,256]{3,2,1,0:T(8,128)S(1)}, f32[1,2,8,256]{3,2,1,0:T(8,128)S(1)}, u32[]{:S(2)}, u32[]{:S(2)}) collective-permute-start(f32[1,2,8,256]{3,2,1,0:T(8,128)S(1)} %get-tuple-element.23), channel_id=1, source_target_pairs={{0,8},{8,0},{16,24},{24,16},{1,9},{9,1},{17,25},{25,17},{2,10},{10... | collective-permute-start | bytes 49160 | tf_op jit(solution)/shard_map/ppermute | solution.py:194
  4.8 1.7 %collective-permute-done = f32[1,2,8,256]{3,2,1,0:T(8,128)S(1)} collective-permute-done((f32[1,2,8,256]{3,2,1,0:T(8,128)S(1)}, f32[1,2,8,256]{3,2,1,0:T(8,128)S(1)}, u32[]{:S(2)}, u32[]{:S(2)}) %collective-permute-start) | collective-permute-done | bytes 16416 | tf_op jit(solution)/shard_map/ppermute | solution.py:194
  6.5 3.0 %collective-permute-start.1 = (f32[2,2,8,256]{3,2,1,0:T(8,128)S(1)}, f32[2,2,8,256]{3,2,1,0:T(8,128)S(1)}, u32[]{:S(2)}, u32[]{:S(2)}) collective-permute-start(f32[2,2,8,256]{3,2,1,0:T(8,128)S(1)} %get-tuple-element.52.gate), channel_id=1, source_target_pairs={{0,16},{8,24},{16,0},{24,8},{1,17},{9,25},{17,1},{25,9},{2,18},{10... | collective-permute-start | bytes 98312 | tf_op jit(solution)/shard_map/ppermute | solution.py:194
  9.6 1.9 %collective-permute-done.1 = f32[2,2,8,256]{3,2,1,0:T(8,128)S(1)} collective-permute-done((f32[2,2,8,256]{3,2,1,0:T(8,128)S(1)}, f32[2,2,8,256]{3,2,1,0:T(8,128)S(1)}, u32[]{:S(2)}, u32[]{:S(2)}) %collective-permute-start.1) | collective-permute-done | bytes 32800 | tf_op jit(solution)/shard_map/ppermute | solution.py:194
  11.5 1.9 %collective-permute-start.2 = (f32[4,2,8,256]{3,2,1,0:T(8,128)S(1)}, f32[4,2,8,256]{3,2,1,0:T(8,128)S(1)}, u32[]{:S(2)}, u32[]{:S(2)}) collective-permute-start(f32[4,2,8,256]{3,2,1,0:T(8,128)S(1)} %get-tuple-element.48.gate), channel_id=1, source_target_pairs={{0,2},{2,0},{4,6},{6,4},{1,3},{3,1},{5,7},{7,5},{8,10},{10,8},{12,... | collective-permute-start | bytes 196616 | tf_op jit(solution)/shard_map/ppermute | solution.py:194
  13.4 2.4 %collective-permute-done.2 = f32[4,2,8,256]{3,2,1,0:T(8,128)S(1)} collective-permute-done((f32[4,2,8,256]{3,2,1,0:T(8,128)S(1)}, f32[4,2,8,256]{3,2,1,0:T(8,128)S(1)}, u32[]{:S(2)}, u32[]{:S(2)}) %collective-permute-start.2) | collective-permute-done | bytes 65568 | tf_op jit(solution)/shard_map/ppermute | solution.py:194
  15.8 1.9 %collective-permute-start.3 = (f32[8,2,8,256]{3,2,1,0:T(8,128)S(1)}, f32[8,2,8,256]{3,2,1,0:T(8,128)S(1)}, u32[]{:S(2)}, u32[]{:S(2)}) collective-permute-start(f32[8,2,8,256]{3,2,1,0:T(8,128)S(1)} %get-tuple-element.44.gate), channel_id=1, source_target_pairs={{0,4},{2,6},{4,0},{6,2},{1,5},{3,7},{5,1},{7,3},{8,12},{10,14},{12... | collective-permute-start | bytes 393224 | tf_op jit(solution)/shard_map/ppermute | solution.py:194
  17.7 0.3 shard_map.78
  18.0 0.1 pad_add_fusion.here_ref
  18.1 1.1 %shard_map.79 = (f32[256,256]{1,0:T(8,128)S(1)}, bf16[2,256,256]{2,1,0:T(8,128)(2,1)S(1)}, bf16[2,256,256]{2,1,0:T(8,128)(2,1)S(1)}) custom-call(f32[2,2,8,256]{3,2,1,0:T(8,128)S(1)} %get-tuple-element.52.gate, f32[256,256]{1,0:T(8,128)S(1)} %get-tuple-element.32.in_ref), custom_call_target="tpu_custom_call" | custom-call | tf_op jit(solution)/shard_map/pallas_call | solution.py:243
  19.2 1.1 %shard_map.80 = (f32[256,256]{1,0:T(8,128)S(1)}, bf16[2,256,256]{2,1,0:T(8,128)(2,1)S(1)}, bf16[2,256,256]{2,1,0:T(8,128)(2,1)S(1)}) custom-call(f32[4,2,8,256]{3,2,1,0:T(8,128)S(1)} %get-tuple-element.48.gate, f32[256,256]{1,0:T(8,128)S(1)} %get-tuple-element.34.in_ref), custom_call_target="tpu_custom_call" | custom-call | tf_op jit(solution)/shard_map/pallas_call | solution.py:243
  20.3 1.8 %shard_map.81 = (f32[256,256]{1,0:T(8,128)}, bf16[2,256,256]{2,1,0:T(8,128)(2,1)S(1)}, bf16[2,256,256]{2,1,0:T(8,128)(2,1)S(1)}) custom-call(f32[8,2,8,256]{3,2,1,0:T(8,128)S(1)} %get-tuple-element.44.gate, f32[256,256]{1,0:T(8,128)S(1)} %get-tuple-element.36.in_ref), custom_call_target="tpu_custom_call" | custom-call | tf_op jit(solution)/shard_map/pallas_call | solution.py:243
  22.1 0.0 collective-permute-done.3
  22.1 0.6 %shard_map.82 = (f32[16,128]{1,0:T(8,128)S(1)}, f32[16,128]{1,0:T(8,128)S(1)}) custom-call(s32[2]{0:T(128)S(1)} %pad_add_fusion.here_ref, f32[16,2,8,256]{3,2,1,0:T(8,128)S(1)} %constant_dynamic-update-slice_fusion.9.data_ref, f32[8,256]{1,0:T(8,128)S(1)} %get-tuple-element.26.rows_ref, f32[256,128]{1,0:T(8,128)S(1)} %get-tuple-element.27.kept_ref, ...), custom_call_target="tpu_custom_call" | custom-call | tf_op jit(solution)/shard_map/pallas_call | solution.py:261
  22.7 6.2 %collective-permute-start.4 = (f32[16,128]{1,0:T(8,128)S(1)}, f32[16,128]{1,0:T(8,128)S(1)}, u32[]{:S(2)}, u32[]{:S(2)}) collective-permute-start(f32[16,128]{1,0:T(8,128)S(1)} %get-tuple-element.43), channel_id=1, source_target_pairs={{0,1},{1,0},{2,3},{3,2},{4,5},{5,4},{6,7},{7,6},{8,9},{9,8},{10,11... | collective-permute-start | bytes 24584 | tf_op jit(solution)/shard_map/ppermute | solution.py:275
  28.9 0.8 %collective-permute-done.4 = f32[16,128]{1,0:T(8,128)S(1)} collective-permute-done((f32[16,128]{1,0:T(8,128)S(1)}, f32[16,128]{1,0:T(8,128)S(1)}, u32[]{:S(2)}, u32[]{:S(2)}) %collective-permute-start.4) | collective-permute-done | bytes 8224 | tf_op jit(solution)/shard_map/ppermute | solution.py:275
  29.7 0.6 %fusion = (f32[8,128]{1,0:T(8,128)}, f32[8,128]{1,0:T(8,128)}) fusion(f32[16,128]{1,0:T(8,128)S(1)} %broadcast_select_fusion), kind=kLoop, calls=%fused_computation.16 | loop fusion | bytes 16384 | tf_op jit(solution)/shard_map/slice | solution.py:277
  (6 shorter events, 0.0 us)
Async XLA Ops:
  1.7 4.8 %collective-permute-start = (f32[1,2,8,256]{3,2,1,0:T(8,128)S(1)}, f32[1,2,8,256]{3,2,1,0:T(8,128)S(1)}, u32[]{:S(2)}, u32[]{:S(2)}) collective-permute-start(f32[1,2,8,256]{3,2,1,0:T(8,128)S(1)} %get-tuple-element.23), channel_id=1, source_target_pairs={{0,8},{8,0},{16,24},{24,16},{1,9},{9,1},{17,25},{25,17},{2,10},{10... | collective-permute-start | bytes 49160 | tf_op jit(solution)/shard_map/ppermute | solution.py:194
  6.5 4.9 %collective-permute-start.1 = (f32[2,2,8,256]{3,2,1,0:T(8,128)S(1)}, f32[2,2,8,256]{3,2,1,0:T(8,128)S(1)}, u32[]{:S(2)}, u32[]{:S(2)}) collective-permute-start(f32[2,2,8,256]{3,2,1,0:T(8,128)S(1)} %get-tuple-element.52.gate), channel_id=1, source_target_pairs={{0,16},{8,24},{16,0},{24,8},{1,17},{9,25},{17,1},{25,9},{2,18},{10... | collective-permute-start | bytes 98312 | tf_op jit(solution)/shard_map/ppermute | solution.py:194
  11.5 4.3 %collective-permute-start.2 = (f32[4,2,8,256]{3,2,1,0:T(8,128)S(1)}, f32[4,2,8,256]{3,2,1,0:T(8,128)S(1)}, u32[]{:S(2)}, u32[]{:S(2)}) collective-permute-start(f32[4,2,8,256]{3,2,1,0:T(8,128)S(1)} %get-tuple-element.48.gate), channel_id=1, source_target_pairs={{0,2},{2,0},{4,6},{6,4},{1,3},{3,1},{5,7},{7,5},{8,10},{10,8},{12,... | collective-permute-start | bytes 196616 | tf_op jit(solution)/shard_map/ppermute | solution.py:194
  15.8 6.3 %collective-permute-start.3 = (f32[8,2,8,256]{3,2,1,0:T(8,128)S(1)}, f32[8,2,8,256]{3,2,1,0:T(8,128)S(1)}, u32[]{:S(2)}, u32[]{:S(2)}) collective-permute-start(f32[8,2,8,256]{3,2,1,0:T(8,128)S(1)} %get-tuple-element.44.gate), channel_id=1, source_target_pairs={{0,4},{2,6},{4,0},{6,2},{1,5},{3,7},{5,1},{7,3},{8,12},{10,14},{12... | collective-permute-start | bytes 393224 | tf_op jit(solution)/shard_map/ppermute | solution.py:194
  22.7 7.1 %collective-permute-start.4 = (f32[16,128]{1,0:T(8,128)S(1)}, f32[16,128]{1,0:T(8,128)S(1)}, u32[]{:S(2)}, u32[]{:S(2)}) collective-permute-start(f32[16,128]{1,0:T(8,128)S(1)} %get-tuple-element.43), channel_id=1, source_target_pairs={{0,1},{1,0},{2,3},{3,2},{4,5},{5,4},{6,7},{7,6},{8,9},{9,8},{10,11... | collective-permute-start | bytes 24584 | tf_op jit(solution)/shard_map/ppermute | solution.py:275

commit v3 on v2

v3 whole, which is shorter than its diff:
```python
import functools
import jax
import jax.numpy as jnp
from jax import lax
from jax.experimental import pallas as pl
from jax.experimental.pallas import tpu as pltpu
from jax.sharding import PartitionSpec as P

HIGHEST = lax.Precision.HIGHEST
F32 = jnp.float32
BF16 = jnp.bfloat16
ROWS = 8
LANES = 128
BITS = 4
VMEM = pl.BlockSpec(memory_space=pltpu.VMEM)
HBM = pl.BlockSpec(memory_space=pltpu.HBM)


def params(mib):
    return pltpu.CompilerParams(vmem_limit_bytes=mib * 2**20)


def split(x):
    high = x.astype(BF16)
    return high, (x - high.astype(F32)).astype(BF16)


def dot3(x, high, low):
    x_high, x_low = split(x)
    n = x.shape[0]
    both = jnp.dot(jnp.concatenate([x_high, x_low], 0), high, preferred_element_type=F32)
    return both[:n] + (both[n:] + jnp.dot(x_high, low, preferred_element_type=F32))


def down_sum(x):
    for shift in (4, 2, 1):
        x = x + pltpu.roll(x, shift, 0)
    return x


def load_kernel(obs_hbm, mask_hbm, data_ref, mask_ref, sems):
    copies = (
        pltpu.make_async_copy(obs_hbm, data_ref.at[0, 0], sems.at[0]),
        pltpu.make_async_copy(mask_hbm, mask_ref, sems.at[1]),
    )
    for copy in copies:
        copy.start()
    for copy in copies:
        copy.wait()
    data_ref[0, 1] = mask_ref[...].astype(F32)


def setup_kernel(
    t_hbm, scale_hbm, gains_hbm, mean_hbm,
    t_ref, in_ref, power_ref, high_ref, low_ref, sems,
):
    sources = (t_hbm, scale_hbm, gains_hbm, mean_hbm)
    targets = (t_ref, in_ref.at[0], in_ref.at[1], in_ref.at[2])
    copies = [
        pltpu.make_async_copy(source, target, sems.at[k])
        for k, (source, target) in enumerate(zip(sources, targets))
    ]
    for copy in copies:
        copy.start()
    for copy in copies:
        copy.wait()
    power = t_ref[...] * in_ref[0]
    power_ref[...] = power
    high_ref[0], low_ref[0] = split(power)


def layout_kernel(t_ref, in_ref, tt_ref, th_ref, tl_ref, rows_ref, kept_ref):
    width = t_ref.shape[0]
    scale, gains = in_ref[0], in_ref[1]
    t = t_ref[...]
    t_t = jnp.transpose(t)
    tt_ref[...] = t_t
    th_ref[...], tl_ref[...] = split(t_t)
    rows_ref[0:1] = gains
    rows_ref[1:2] = in_ref[2]
    rows_ref[2:3] = 1.0 - scale * jnp.sum(t * t, axis=0, keepdims=True)
    kept = jnp.transpose(jnp.broadcast_to(1.0 - gains, (ROWS, width)))
    kept_ref[...] = jnp.broadcast_to(kept[:, :1], (width, LANES))


def power_kernel(exact, in_ref, power_ref, high_ref, low_ref):
    power = in_ref[...]
    high, low = split(power)
    for k in range(high_ref.shape[0]):
        if exact:
            power = jnp.dot(power, power, precision=HIGHEST, preferred_element_type=F32)
        else:
            power = dot3(power, high, low)
        high, low = split(power)
        high_ref[k], low_ref[k] = high, low
    power_ref[...] = power


def smoother_kernel(steps, data_ref, rows_ref, kept_ref, t_ref, tt_ref, th_ref, tl_ref, *refs):
    highs, lows = refs[: len(steps)], refs[len(steps) : 2 * len(steps)]
    send_ref, mine_ref, bits_ref, retain_ref, force_ref, f_ref, s_ref = refs[2 * len(steps) :]
    blocks = data_ref.shape[0]
    width = data_ref.shape[-1]
    days = blocks * ROWS
    here = lax.axis_index("grp") * lax.axis_size("seg") + lax.axis_index("seg")
    pair = lax.axis_index("pair")
    half = width // 2
    tiles = width // ROWS
    powers = [(high, low, k) for high, low, n in zip(highs, lows, steps) for k in range(n)]

    def advance(x, k):
        high, low, at = powers[k]
        return dot3(x, high[at], low[at])

    @pl.when(pair > 0)
    def work():
        row = lax.broadcasted_iota(jnp.int32, (ROWS, width), 0)
        gains = rows_ref[0:1]
        group = min(ROWS, blocks)

        def prepare(word, carry):
            packed = jnp.zeros((ROWS, width), jnp.int32)
            for q in range(group):
                mask = data_ref[word * group + q, 1]
                even = jnp.where((row & 1) == 0, mask, 0.0).astype(jnp.int32)
                packed = packed | (even << ((row >> 1) + BITS * q))
            for shift in (4, 2):
                packed = packed | pltpu.roll(packed, shift, 0)
            bits_ref[word] = jnp.broadcast_to(jnp.transpose(packed)[:, :1], (width, LANES))
            return carry

        lax.fori_loop(0, blocks // group, prepare, 0)
        f_ref[...] = jnp.zeros(f_ref.shape, F32)
        mean = rows_ref[1:2]
        f_ref[ROWS - 1 : ROWS] = mean

        def factors(block):
            at = lax.bitwise_xor(block, here)
            observed = data_ref[at, 1] * gains
            retain = 1.0 - observed
            force = observed * data_ref[at, 0]
            ahead = pltpu.roll(dot3(force, th_ref[...], tl_ref[...]), 1, 0)
            return retain, jnp.where((row & 1) == 1, retain * ahead, 0.0) + force

        def forward(block, carry):
            x, retain, force = carry
            following = factors(jnp.minimum(block + 1, blocks - 1))
            retain_ref[block], force_ref[block] = retain, force
            at = lax.bitwise_xor(block, here)
            word, first = at // group, 31 - BITS * (at % group)
            out = jnp.zeros((ROWS, width), F32)
            for k in range(0, ROWS, 2):
                left, right = x[:, :half], x[:, half:]
                total_left = jnp.zeros((ROWS, half), F32)
                total_right = total_left
                for j in range(tiles):
                    at = slice(ROWS * j, ROWS * (j + 1))
                    product = t_ref[at, :half] * left + t_ref[at, half:] * right
                    u = jnp.broadcast_to(jnp.sum(product, axis=1, keepdims=True), (ROWS, half))
                    seen = bits_ref[word, at] << (first - k // 2)
                    u = jnp.where(seen < 0, u * kept_ref[at], u)
                    total_left = total_left + tt_ref[at, :half] * u
                    total_right = total_right + tt_ref[at, half:] * u
                z = down_sum(jnp.concatenate([total_left, total_right], 1))
                x = retain[k + 1 : k + 2] * z + force[k + 1 : k + 2]
                out = jnp.where(row == k + 1, x, out)
            f_ref[pl.ds(pl.multiple_of(ROWS * block + ROWS, ROWS), ROWS)] = out
            return (x, *following)

        lax.fori_loop(0, blocks, forward, (jnp.broadcast_to(mean, (ROWS, width)), *factors(0)))
        every = pl.ds(ROWS, days)
        ahead = dot3(f_ref[pl.ds(ROWS - 1, days + ROWS)], th_ref[...], tl_ref[...])
        boundary = ahead[days:]
        even_days = retain_ref[...].reshape(days, width) * ahead[:days] + force_ref[...].reshape(days, width)
        day = lax.broadcasted_iota(jnp.int32, (days, width), 0)
        filtered = jnp.where((day & 1) == 0, even_days, f_ref[every])
        f_ref[every] = filtered
        s_ref[pl.ds(0, days)] = filtered * rows_ref[2:3]
        s_ref[pl.ds(days, ROWS)] = jnp.where(row == 0, boundary, 0.0)
        s_ref[pl.ds(days + ROWS, days - ROWS)] = jnp.zeros((days - ROWS, width), F32)
        entering = advance(boundary, 3)
        step, k = 1, 0
        while step < ROWS:
            s_ref[pl.ds(0, days)] = s_ref[pl.ds(0, days)] + advance(s_ref[pl.ds(step, days)], k)
            step, k = 2 * step, k + 1
        tail = pl.ds(days - ROWS, ROWS)
        s_ref[tail] = s_ref[tail] + jnp.where(row == 0, entering, 0.0)
        s_ref[pl.ds(days, ROWS)] = jnp.zeros((ROWS, width), F32)
        base = pl.multiple_of(here * ROWS, ROWS)
        k = len(powers) - 1
        step = days // 2
        while step >= ROWS:
            s_ref[pl.ds(base, step)] = s_ref[pl.ds(base, step)] + advance(s_ref[pl.ds(base + step, step)], k)
            step, k = step // 2, k - 1
        own_filtered = f_ref[pl.ds(base + ROWS, ROWS)]
        own_smoothed = s_ref[pl.ds(base, ROWS)]
        send_ref[:ROWS], mine_ref[:ROWS] = own_filtered[:, :half], own_filtered[:, half:]
        send_ref[ROWS:], mine_ref[ROWS:] = own_smoothed[:, :half], own_smoothed[:, half:]

    @pl.when(pair == 0)
    def idle():
        send_ref[...] = jnp.zeros(send_ref.shape, F32)
        mine_ref[...] = jnp.zeros(mine_ref.shape, F32)


def swap(x, axis, flip):
    return lax.ppermute(x, axis, [(i, i ^ flip) for i in range(lax.axis_size(axis))])


def shape(*dims, dtype=F32):
    return jax.ShapeDtypeStruct(dims, dtype)


def hops(mesh_shape):
    return [(axis, 1 << k) for axis in ("seg", "grp") for k in range(mesh_shape[axis].bit_length() - 1)]


def squarings(count):
    rest = max(0, count - 2)
    chain = []
    for k in range(1, count - 1):
        take = min(2, rest)
        rest -= take
        if take:
            chain.append((k, take))
    return chain + [(count - 1, 4 + rest)]


def keep_in_hbm(x):
    return pltpu.with_memory_space_constraint(x, pltpu.HBM)


def shards(observations, masks, gains, transition, smoother_scale, initial_mean):
    width = transition.shape[0]
    sizes = {axis: lax.axis_size(axis) for axis in ("seg", "grp")}
    blocks = sizes["seg"] * sizes["grp"]
    days = blocks * ROWS
    half = width // 2
    flips = hops(sizes)
    data = pl.pallas_call(
        load_kernel,
        out_shape=shape(1, 2, ROWS, width),
        in_specs=[HBM] * 2,
        out_specs=VMEM,
        scratch_shapes=[pltpu.VMEM((ROWS, width), jnp.int32), pltpu.SemaphoreType.DMA((2,))],
        compiler_params=params(4),
    )(keep_in_hbm(observations), keep_in_hbm(masks))
    t, vectors, power, high, low = pl.pallas_call(
        setup_kernel,
        out_shape=(
            shape(width, width), shape(3, 1, width), shape(width, width),
            shape(1, width, width, dtype=BF16), shape(1, width, width, dtype=BF16),
        ),
        in_specs=[HBM] * 4,
        out_specs=[VMEM] * 5,
        scratch_shapes=[pltpu.SemaphoreType.DMA((4,))],
        compiler_params=params(8),
    )(*(keep_in_hbm(x) for x in (transition, smoother_scale[None, :], gains[None, :], initial_mean[None, :])))
    tt, th, tl, rows, kept = pl.pallas_call(
        layout_kernel,
        out_shape=(
            shape(width, width), shape(width, width, dtype=BF16), shape(width, width, dtype=BF16),
            shape(ROWS, width), shape(width, LANES),
        ),
        in_specs=[VMEM] * 2,
        out_specs=[VMEM] * 5,
        compiler_params=params(8),
    )(t, vectors)
    highs, lows, steps = [high], [low], [1]
    for k, count in squarings(len(flips)):
        power, high, low = pl.pallas_call(
            functools.partial(power_kernel, k + 1 < len(flips)),
            out_shape=(
                shape(width, width),
                shape(count, width, width, dtype=BF16),
                shape(count, width, width, dtype=BF16),
            ),
            in_specs=[VMEM],
            out_specs=[VMEM] * 3,
            compiler_params=params(8),
        )(power)
        highs.append(high)
        lows.append(low)
        steps.append(count)
    for axis, flip in flips[:-2]:
        other = swap(data, axis, flip)
        data = jnp.concatenate([data, other], 0)
    first, last = len(flips) - 2, len(flips) - 1
    near = swap(data, *flips[first])
    side = swap(data, *flips[last])
    corner = swap(near, *flips[last])
    data = jnp.concatenate([data, near, side, corner], 0)
    pair = lax.axis_index("pair")
    send, mine = pl.pallas_call(
        functools.partial(smoother_kernel, steps),
        out_shape=(shape(2 * ROWS, half),) * 2,
        in_specs=[VMEM] * (7 + 2 * len(steps)),
        out_specs=[VMEM] * 2,
        scratch_shapes=[
            pltpu.VMEM((max(1, blocks // ROWS), width, LANES), jnp.int32),
            pltpu.VMEM((blocks, ROWS, width), F32),
            pltpu.VMEM((blocks, ROWS, width), F32),
            pltpu.VMEM((days + 2 * ROWS, width), F32),
            pltpu.VMEM((2 * days, width), F32),
        ],
        compiler_params=params(12 + blocks // 8),
    )(data, rows, kept, t, tt, th, tl, *highs, *lows)
    got = lax.ppermute(send, "pair", [(0, 1), (1, 0)])
    out = jnp.where(pair == 1, mine, got)
    return out[:ROWS], out[ROWS:]


def solution(mesh):
    return jax.shard_map(
        shards,
        mesh=mesh,
        in_specs=(P(("grp", "seg"), None), P(("grp", "seg"), None), P(), P(), P(), P()),
        out_specs=(P(("grp", "seg"), "pair"), P(("grp", "seg"), "pair")),
        check_vma=False,
    )
```

time: 30.5 us -> 30.6 us (level)
  starting transfers between devices: 16.2 us -> 17.2 us
  Pallas kernels: 5.85 us -> 5.16 us
  waiting for transfers between devices: 6.88 us -> 6.55 us
    ppermute x4 -> x5, starting transfers between devices: 9.96 us -> 10.8 us  [swap(): lax.ppermute(x, axis, [(i, i ^ flip) for i in range(lax.axis_size(axis))])]
    pallas_call x1, Pallas kernels: 0.57 us -> 0.01 us  [shards(): pl.pallas_call(functools.partial(smoother_kernel, steps), out_shape=(shap...]
    ppermute x4 -> x5, waiting for transfers between devices: 6.05 us -> 5.72 us  [swap(): lax.ppermute(x, axis, [(i, i ^ flip) for i in range(lax.axis_size(axis))])]
  transfers between devices with their start and end apart: 5 -> 6, of which waited for: 4 -> 4; matrix products, arithmetic and copies ran while one was open for 0% -> 0% of each run, Pallas kernels for 14% -> 15%
where the time goes in v3:
time: 30.6 us; the launch traced here: 30.3 us
  starting transfers between devices  17.2 us (56%)
  waiting for transfers between devices  6.55 us (21%)
  Pallas kernels  5.16 us (17%)
  between operations  0.7 us (2%)
  local copies, waits for them, and re-layouts  0.63 us (2%)
    ppermute x5, starting transfers between devices, swap(): lax.ppermute(x, axis, [(i, i ^ flip) for i in range(lax.axis_size(axis))])  10.8 us
    ppermute x1, starting transfers between devices, shards(): got = lax.ppermute(send, 'pair', [(0, 1), (1, 0)])  6.45 us
    ppermute x5, waiting for transfers between devices, swap(): lax.ppermute(x, axis, [(i, i ^ flip) for i in range(lax.axis_size(axis))])  5.72 us
    pallas_call x2, Pallas kernels, shards(): pl.pallas_call(functools.partial(power_kernel, k + 1 < len(flips)), out_s...  3.11 us
    pallas_call x1, Pallas kernels, shards(): pl.pallas_call(setup_kernel, out_shape=(shape(width, width), shape(3, 1,...  1.05 us
    ppermute x1, waiting for transfers between devices, shards(): got = lax.ppermute(send, 'pair', [(0, 1), (1, 0)])  0.83 us
    pallas_call x1, Pallas kernels, shards(): pl.pallas_call(load_kernel, out_shape=shape(1, 2, ROWS, width), in_specs=...  0.73 us
  transfers between devices with their start and end apart: 6, of which 4 were waited for; matrix products, arithmetic and copies ran while one was open for 0% of the time, Pallas kernels for 15%

profile of v3, /device:TPU:0, one launch (start us, length us, event | category | flops | bytes accessed | tf_op | source)
XLA Modules:
  0.0 30.3 jit_solution(7365843054183736639)
XLA Ops:
  0.6 0.7 %shard_map.77 = f32[1,2,8,256]{3,2,1,0:T(8,128)S(1)} custom-call(f32[8,256]{1,0:T(8,128)} %obs_hbm.1, s32[8,256]{1,0:T(8,128)} %mask_hbm.1), custom_call_target="tpu_custom_call" | custom-call | tf_op jit(solution)/shard_map/pallas_call | solution.py:240
  1.4 3.1 %collective-permute-start = (f32[1,2,8,256]{3,2,1,0:T(8,128)S(1)}, f32[1,2,8,256]{3,2,1,0:T(8,128)S(1)}, u32[]{:S(2)}, u32[]{:S(2)}) collective-permute-start(f32[1,2,8,256]{3,2,1,0:T(8,128)S(1)} %shard_map.77), channel_id=1, source_target_pairs={{0,8},{8,0},{16,24},{24,16},{1,9},{9,1},{17,25},{25,17},{2,10},{10... | collective-permute-start | bytes 49160 | tf_op jit(solution)/shard_map/ppermute | solution.py:207
  4.5 1.0 %shard_map.78 = (f32[256,256]{1,0:T(8,128)S(1)}, f32[3,1,256]{2,1,0:T(1,128)S(1)}, f32[256,256]{1,0:T(8,128)S(1)}, bf16[1,256,256]{2,1,0:T(8,128)(2,1)S(1)}, bf16[1,256,256]{2,1,0:T(8,128)(2,1)S(1)}) custom-call(f32[256,256]{1,0:T(8,128)} %t_hbm.1, f32[1,256]{1,0:T(1,128)} %bitcast.3, f32[1,256]{1,0:T(1,128)} %bitcast.4, f32[1,256]{1,0:T(1,128)} %bitcast.5), custom_call_target="tpu_custom_call" | custom-call | tf_op jit(solution)/shard_map/pallas_call | solution.py:248
  5.5 1.1 %shard_map.80 = (f32[256,256]{1,0:T(8,128)S(1)}, bf16[2,256,256]{2,1,0:T(8,128)(2,1)S(1)}, bf16[2,256,256]{2,1,0:T(8,128)(2,1)S(1)}) custom-call(f32[256,256]{1,0:T(8,128)S(1)} %get-tuple-element.27.in_ref), custom_call_target="tpu_custom_call" | custom-call | tf_op jit(solution)/shard_map/pallas_call | solution.py:271
  6.6 2.0 %shard_map.81 = (f32[256,256]{1,0:T(8,128)}, bf16[4,256,256]{2,1,0:T(8,128)(2,1)S(1)}, bf16[4,256,256]{2,1,0:T(8,128)(2,1)S(1)}) custom-call(f32[256,256]{1,0:T(8,128)S(1)} %get-tuple-element.29.in_ref), custom_call_target="tpu_custom_call" | custom-call | tf_op jit(solution)/shard_map/pallas_call | solution.py:271
  8.7 0.3 shard_map.79
  8.9 0.0 collective-permute-done
  9.0 2.7 %collective-permute-start.1 = (f32[2,2,8,256]{3,2,1,0:T(8,128)S(1)}, f32[2,2,8,256]{3,2,1,0:T(8,128)S(1)}, u32[]{:S(2)}, u32[]{:S(2)}) collective-permute-start(f32[2,2,8,256]{3,2,1,0:T(8,128)S(1)} %pad_maximum_fusion.1), channel_id=1, source_target_pairs={{0,16},{8,24},{16,0},{24,8},{1,17},{9,25},{17,1},{25,9},{2,18},{10... | collective-permute-start | bytes 98312 | tf_op jit(solution)/shard_map/ppermute | solution.py:207
  11.6 2.2 %collective-permute-done.1 = f32[2,2,8,256]{3,2,1,0:T(8,128)S(1)} collective-permute-done((f32[2,2,8,256]{3,2,1,0:T(8,128)S(1)}, f32[2,2,8,256]{3,2,1,0:T(8,128)S(1)}, u32[]{:S(2)}, u32[]{:S(2)}) %collective-permute-start.1) | collective-permute-done | bytes 32800 | tf_op jit(solution)/shard_map/ppermute | solution.py:207
  13.8 1.7 %collective-permute-start.2 = (f32[4,2,8,256]{3,2,1,0:T(8,128)S(1)}, f32[4,2,8,256]{3,2,1,0:T(8,128)S(1)}, u32[]{:S(2)}, u32[]{:S(2)}) collective-permute-start(f32[4,2,8,256]{3,2,1,0:T(8,128)S(1)} %pad_maximum_fusion), channel_id=1, source_target_pairs={{0,2},{2,0},{4,6},{6,4},{1,3},{3,1},{5,7},{7,5},{8,10},{10,8},{12,... | collective-permute-start | bytes 196616 | tf_op jit(solution)/shard_map/ppermute | solution.py:207
  15.6 1.5 %collective-permute-start.3 = (f32[4,2,8,256]{3,2,1,0:T(8,128)S(1)}, f32[4,2,8,256]{3,2,1,0:T(8,128)S(1)}, u32[]{:S(2)}, u32[]{:S(2)}) collective-permute-start(f32[4,2,8,256]{3,2,1,0:T(8,128)S(1)} %pad_maximum_fusion), channel_id=1, source_target_pairs={{0,4},{2,6},{4,0},{6,2},{1,5},{3,7},{5,1},{7,3},{8,12},{10,14},{12... | collective-permute-start | bytes 196616 | tf_op jit(solution)/shard_map/ppermute | solution.py:207
  17.1 1.0 %collective-permute-done.2 = f32[4,2,8,256]{3,2,1,0:T(8,128)S(1)} collective-permute-done((f32[4,2,8,256]{3,2,1,0:T(8,128)S(1)}, f32[4,2,8,256]{3,2,1,0:T(8,128)S(1)}, u32[]{:S(2)}, u32[]{:S(2)}) %collective-permute-start.2) | collective-permute-done | bytes 65568 | tf_op jit(solution)/shard_map/ppermute | solution.py:207
  18.1 1.8 %collective-permute-start.4 = (f32[4,2,8,256]{3,2,1,0:T(8,128)S(1)}, f32[4,2,8,256]{3,2,1,0:T(8,128)S(1)}, u32[]{:S(2)}, u32[]{:S(2)}) collective-permute-start(f32[4,2,8,256]{3,2,1,0:T(8,128)S(1)} %collective-permute-done.2), channel_id=1, source_target_pairs={{0,4},{2,6},{4,0},{6,2},{1,5},{3,7},{5,1},{7,3},{8,12},{10,14},{12... | collective-permute-start | bytes 196616 | tf_op jit(solution)/shard_map/ppermute | solution.py:207
  19.9 0.0 collective-permute-done.3
  19.9 2.5 %collective-permute-done.4 = f32[4,2,8,256]{3,2,1,0:T(8,128)S(1)} collective-permute-done((f32[4,2,8,256]{3,2,1,0:T(8,128)S(1)}, f32[4,2,8,256]{3,2,1,0:T(8,128)S(1)}, u32[]{:S(2)}, u32[]{:S(2)}) %collective-permute-start.4) | collective-permute-done | bytes 65568 | tf_op jit(solution)/shard_map/ppermute | solution.py:207
  22.4 6.5 %collective-permute-start.5 = (f32[16,128]{1,0:T(8,128)S(1)}, f32[16,128]{1,0:T(8,128)S(1)}, u32[]{:S(2)}, u32[]{:S(2)}) collective-permute-start(f32[16,128]{1,0:T(8,128)S(1)} %get-tuple-element.35), channel_id=1, source_target_pairs={{0,1},{1,0},{2,3},{3,2},{4,5},{5,4},{6,7},{7,6},{8,9},{9,8},{10,11... | collective-permute-start | bytes 24584 | tf_op jit(solution)/shard_map/ppermute | solution.py:308
  28.8 0.8 %collective-permute-done.5 = f32[16,128]{1,0:T(8,128)S(1)} collective-permute-done((f32[16,128]{1,0:T(8,128)S(1)}, f32[16,128]{1,0:T(8,128)S(1)}, u32[]{:S(2)}, u32[]{:S(2)}) %collective-permute-start.5) | collective-permute-done | bytes 8224 | tf_op jit(solution)/shard_map/ppermute | solution.py:308
  29.7 0.6 %fusion = (f32[8,128]{1,0:T(8,128)}, f32[8,128]{1,0:T(8,128)}) fusion(f32[16,128]{1,0:T(8,128)S(1)} %broadcast_select_fusion), kind=kLoop, calls=%fused_computation.9 | loop fusion | bytes 16384 | tf_op jit(solution)/shard_map/slice | solution.py:310
  (10 shorter events, 0.0 us)
Async XLA Ops:
  1.4 7.6 %collective-permute-start = (f32[1,2,8,256]{3,2,1,0:T(8,128)S(1)}, f32[1,2,8,256]{3,2,1,0:T(8,128)S(1)}, u32[]{:S(2)}, u32[]{:S(2)}) collective-permute-start(f32[1,2,8,256]{3,2,1,0:T(8,128)S(1)} %shard_map.77), channel_id=1, source_target_pairs={{0,8},{8,0},{16,24},{24,16},{1,9},{9,1},{17,25},{25,17},{2,10},{10... | collective-permute-start | bytes 49160 | tf_op jit(solution)/shard_map/ppermute | solution.py:207
  9.0 4.9 %collective-permute-start.1 = (f32[2,2,8,256]{3,2,1,0:T(8,128)S(1)}, f32[2,2,8,256]{3,2,1,0:T(8,128)S(1)}, u32[]{:S(2)}, u32[]{:S(2)}) collective-permute-start(f32[2,2,8,256]{3,2,1,0:T(8,128)S(1)} %pad_maximum_fusion.1), channel_id=1, source_target_pairs={{0,16},{8,24},{16,0},{24,8},{1,17},{9,25},{17,1},{25,9},{2,18},{10... | collective-permute-start | bytes 98312 | tf_op jit(solution)/shard_map/ppermute | solution.py:207
  13.8 4.3 %collective-permute-start.2 = (f32[4,2,8,256]{3,2,1,0:T(8,128)S(1)}, f32[4,2,8,256]{3,2,1,0:T(8,128)S(1)}, u32[]{:S(2)}, u32[]{:S(2)}) collective-permute-start(f32[4,2,8,256]{3,2,1,0:T(8,128)S(1)} %pad_maximum_fusion), channel_id=1, source_target_pairs={{0,2},{2,0},{4,6},{6,4},{1,3},{3,1},{5,7},{7,5},{8,10},{10,8},{12,... | collective-permute-start | bytes 196616 | tf_op jit(solution)/shard_map/ppermute | solution.py:207
  15.6 4.3 %collective-permute-start.3 = (f32[4,2,8,256]{3,2,1,0:T(8,128)S(1)}, f32[4,2,8,256]{3,2,1,0:T(8,128)S(1)}, u32[]{:S(2)}, u32[]{:S(2)}) collective-permute-start(f32[4,2,8,256]{3,2,1,0:T(8,128)S(1)} %pad_maximum_fusion), channel_id=1, source_target_pairs={{0,4},{2,6},{4,0},{6,2},{1,5},{3,7},{5,1},{7,3},{8,12},{10,14},{12... | collective-permute-start | bytes 196616 | tf_op jit(solution)/shard_map/ppermute | solution.py:207
  18.1 4.3 %collective-permute-start.4 = (f32[4,2,8,256]{3,2,1,0:T(8,128)S(1)}, f32[4,2,8,256]{3,2,1,0:T(8,128)S(1)}, u32[]{:S(2)}, u32[]{:S(2)}) collective-permute-start(f32[4,2,8,256]{3,2,1,0:T(8,128)S(1)} %collective-permute-done.2), channel_id=1, source_target_pairs={{0,4},{2,6},{4,0},{6,2},{1,5},{3,7},{5,1},{7,3},{8,12},{10,14},{12... | collective-permute-start | bytes 196616 | tf_op jit(solution)/shard_map/ppermute | solution.py:207
  22.4 7.3 %collective-permute-start.5 = (f32[16,128]{1,0:T(8,128)S(1)}, f32[16,128]{1,0:T(8,128)S(1)}, u32[]{:S(2)}, u32[]{:S(2)}) collective-permute-start(f32[16,128]{1,0:T(8,128)S(1)} %get-tuple-element.35), channel_id=1, source_target_pairs={{0,1},{1,0},{2,3},{3,2},{4,5},{5,4},{6,7},{7,6},{8,9},{9,8},{10,11... | collective-permute-start | bytes 24584 | tf_op jit(solution)/shard_map/ppermute | solution.py:308
